TPU v7x, 512 devices: a whole 4x8x8 slice. The times are simulated.
512 devices in a mesh: inst: 8 (over z_hi, core), space: 64 (over z_lo, y, x).
Axes of the slice: x: 4, y: 8, z: 8 (z_hi: 4, z_lo: 2; z = z_hi * 2 + z_lo), core: 2. Of those that a mesh axis runs over, the one named last changes fastest.
Arguments:
- state: float32 [8, 5, 64, 32768], P('inst', None, None, 'space'), may hold values from -6 to 6
- metric: float32 [32768], P('space'), may hold values from 1 to 4
- jacobians: float32 [3, 5, 5], replicated, may hold values from -2.5 to 2.5
- dissipation: float32 [1], replicated, may hold values from 0.5 to 2
- omega: float32 [1], replicated, may hold values from 0.5 to 2
- rotor_angle: float32 [8], P('inst'), may hold values from -3.140625 to 3.140625
- counts: int32 [64], P('space'), may hold values from 384 to 512, as said below
- neighbours: int32 [6, 32768], P(None, 'space'), may hold values from 0 to 639, as said below
- mortar_pairs: int32 [8, 16384], P('inst', 'space'), may hold values from 0 to 16383, as said below
Outputs:
- updated: float32 [8, 5, 64, 32768], P('inst', None, None, 'space')
Inputs may be any that keep to these rules, and one draw needn't show every extreme that they name: Some index of space has all 512 slots live; live slots are the first counts ones of a device. `neighbours`: extended numbering of a device: 64 halo slots from the previous device (its slots 64 to 127), its own 512 slots, 64 from the next device (its slots 0 to 63); every entry names a live element. `mortar_pairs`: each row is a permutation; for each instance there is one device offset, the same for all devices, such that the partners of device p's 256 faces lie on devices p plus that offset and the one after it, counted cyclically.
All inputs are finite; a program needn't handle non-finite values.
Results may differ from a plain program's by a relative error of at most 0.0001.
Values sent between devices are 32-bit elements; how exact they have to be, the bound alone decides.
A program may use at most 64 MiB of HBM per device.

v0:
```python
import math

import jax
import jax.numpy as jnp
import numpy as np
from jax import lax
from jax.sharding import PartitionSpec as P

RIM = 64
MORT = 256


courant_number = 0.5


def padded(cells, sides, width):
    for axis, dim in sides:
        count = lax.axis_size(axis)
        head = lax.slice_in_dim(cells, 0, width, axis=dim)
        tail = lax.slice_in_dim(cells, cells.shape[dim] - width, cells.shape[dim], axis=dim)
        cells = jnp.concatenate(
            [
                lax.ppermute(tail, axis, [(i, (i + 1) % count) for i in range(count)]),
                cells,
                lax.ppermute(head, axis, [((i + 1) % count, i) for i in range(count)]),
            ],
            axis=dim,
        )
    return cells


def shifted(value, axis, steps):
    count = lax.axis_size(axis)
    pairs = [(source, (source + steps) % count) for source in range(count)]
    return lax.ppermute(value, axis, pairs)


def gll_table():
    nodes = np.array([-1.0, -1.0 / math.sqrt(5.0), 1.0 / math.sqrt(5.0), 1.0])
    barycentric = np.array(
        [1.0 / np.prod([nodes[j] - nodes[k] for k in range(4) if k != j]) for j in range(4)]
    )
    derivative = np.zeros((4, 4))
    for i in range(4):
        for j in range(4):
            if i != j:
                derivative[i, j] = barycentric[j] / barycentric[i] / (nodes[i] - nodes[j])
        derivative[i, i] = -np.sum(derivative[i])
    return derivative


def spectral_matrix(inst_count, omega):
    positions = jnp.arange(inst_count)
    offset = positions[:, None] - positions[None, :]
    parity = 1.0 - 2.0 * jnp.mod(offset, 2).astype(jnp.float32)
    safe_offset = jnp.where(offset == 0, 1, offset).astype(jnp.float32)
    angle_value = jnp.pi * safe_offset / inst_count
    cot_value = 0.5 * parity / jnp.tan(angle_value)
    sine_value = jnp.sin(angle_value)
    viscous_value = parity / (2.0 * inst_count * sine_value * sine_value)
    diagonal_value = jnp.float32((inst_count * inst_count + 2.0) / (12.0 * inst_count))
    return jnp.where(offset == 0, diagonal_value, cot_value + viscous_value) * omega[0]


def face_select(face_number):
    direction = face_number // 2
    node_index = 3 * (face_number % 2)
    table = np.zeros((16, 64))
    for first in range(4):
        for second in range(4):
            if direction == 0:
                node = 16 * node_index + 4 * first + second
            elif direction == 1:
                node = 16 * first + 4 * node_index + second
            else:
                node = 16 * first + 4 * second + node_index
            table[4 * first + second, node] = 1.0
    return table


def derivative_tables():
    derivative = gll_table()
    identity = np.eye(4)
    along_a = np.kron(np.kron(derivative, identity), identity)
    along_b = np.kron(np.kron(identity, derivative), identity)
    along_c = np.kron(np.kron(identity, identity), derivative)
    return [along_a, along_b, along_c]


def rotate_rows(trace_rows, angles):
    shaped = trace_rows.reshape(5, 16, trace_rows.shape[-1])
    cosine = jnp.cos(angles[0])
    sine = jnp.sin(angles[0])
    new_two = cosine * shaped[2] - sine * shaped[3]
    new_three = sine * shaped[2] + cosine * shaped[3]
    rotated = jnp.concatenate([shaped[:2], new_two[None], new_three[None], shaped[4:]], axis=0)
    return rotated.reshape(trace_rows.shape)


def shards(
    state, metric, jacobians, dissipation, omega, rotor_angle, counts, neighbours, mortar_pairs
):
    local_elems = state.shape[-1]
    inst_count = lax.axis_size("inst")
    inst_index = lax.axis_index("inst")
    highest = lax.Precision.HIGHEST
    fields_five = np.eye(5)
    selections = [face_select(face_number) for face_number in range(6)]
    select_inner = jnp.asarray(
        np.concatenate([np.kron(fields_five, selections[f]) for f in range(6)], axis=0), jnp.float32
    )
    select_outer = jnp.asarray(
        np.concatenate([np.kron(fields_five, selections[f ^ 1]) for f in range(6)], axis=0),
        jnp.float32,
    )
    tables = derivative_tables()
    volume_matrix = jnp.kron(jacobians[0], jnp.asarray(tables[0], jnp.float32))
    volume_matrix = volume_matrix + jnp.kron(jacobians[1], jnp.asarray(tables[1], jnp.float32))
    volume_matrix = volume_matrix + jnp.kron(jacobians[2], jnp.asarray(tables[2], jnp.float32))
    blocks_list = [-volume_matrix]
    for face_number in range(6):
        lifted = jnp.asarray(selections[face_number].T, jnp.float32)
        normal_sign = 1.0 if face_number % 2 else -1.0
        face_matrix = 0.5 * (
            normal_sign * jnp.kron(jacobians[face_number // 2], lifted)
            - dissipation[0] * jnp.kron(jnp.asarray(fields_five, jnp.float32), lifted)
        )
        blocks_list.append(6.0 * face_matrix)
    operator = jnp.concatenate(blocks_list, axis=1)
    rim_halo = padded(state[..., : 2 * RIM], (("space", 3),), RIM)
    extended = jnp.concatenate([rim_halo[..., :RIM], state, rim_halo[..., 3 * RIM :]], axis=3)
    flat_state = state.reshape(320, local_elems)
    flat_extended = extended.reshape(320, extended.shape[-1])
    inner_traces = jnp.dot(select_inner, flat_state, precision=highest).reshape(6, 80, local_elems)
    outer_all = jnp.dot(select_outer, flat_extended, precision=highest).reshape(
        6, 80, flat_extended.shape[-1]
    )
    outer_traces = jnp.take_along_axis(outer_all, neighbours[:, None, :], axis=2)
    rotor_trace = inner_traces[4][:, 2 * RIM : 2 * RIM + MORT]
    space_count = lax.axis_size("space")
    space_index = lax.axis_index("space")
    following = shifted(rotor_trace, "space", -1)
    window = jnp.concatenate([rotor_trace, following], axis=1)
    relative = jnp.mod(mortar_pairs[0] // MORT - space_index, space_count)
    first_device = relative[0]
    below_device = jnp.mod(first_device - 1, space_count)
    device_offset = jnp.where(jnp.any(relative == below_device), below_device, first_device)
    for bit_number in range((space_count - 1).bit_length()):
        moved = shifted(window, "space", -(1 << bit_number))
        taken = jnp.bitwise_and(jnp.right_shift(device_offset, bit_number), 1) == 1
        window = jnp.where(taken, moved, window)
    local_index = jnp.mod(relative - device_offset, space_count) * MORT + mortar_pairs[0] % MORT
    partner_trace = rotate_rows(jnp.take(window, local_index, axis=1), rotor_angle)
    outer_traces = outer_traces.at[5, :, 2 * RIM : 2 * RIM + MORT].set(partner_trace)
    jumps = (inner_traces - outer_traces).reshape(480, local_elems)
    stacked = jnp.concatenate([flat_state, jumps], axis=0)
    tendency = metric * jnp.dot(operator, stacked, precision=highest)
    matrix = spectral_matrix(inst_count, omega)
    matrix_row = lax.dynamic_slice_in_dim(matrix, inst_index, 1, 0)
    coupling = jnp.einsum(
        "ij,j...->i...",
        matrix_row,
        lax.all_gather(state, "inst", axis=0, tiled=True),
        precision=highest,
    )
    pseudo_step = courant_number / (metric * dissipation[0] + omega[0])
    result = state + pseudo_step * (tendency.reshape(state.shape) - coupling)
    live_mask = jnp.arange(local_elems, dtype=jnp.int32) < counts[0]
    return jnp.where(live_mask, result, jnp.float32(0.0))


def solution(mesh):
    return jax.shard_map(
        shards,
        mesh=mesh,
        in_specs=(
            P("inst", None, None, "space"),
            P("space"),
            P(),
            P(),
            P(),
            P("inst"),
            P("space"),
            P(None, "space"),
            P("inst", "space"),
        ),
        out_specs=P("inst", None, None, "space"),
        check_vma=False,
    )
```

profile of v0, /device:TPU:30, one launch (start us, length us, event | category | flops | bytes accessed | tf_op | source)
XLA Modules:
  0.0 164.4 jit_solution(7486300598190762044)
XLA Ops:
  7.3 1.8 %fusion.36 = (f32[1,5,64,64]{3,2,1,0:T(8,128)}, f32[1,5,64,64]{3,2,1,0:T(8,128)}) fusion(f32[1,5,64,512]{3,2,1,0:T(8,128)} %param.28), kind=kLoop, calls=%fused_computation.105 | loop fusion | bytes 327680 | tf_op jit(solution)/shard_map/slice | solution.py:20
  9.1 4.6 %collective-permute-start = (f32[1,5,64,64]{3,2,1,0:T(8,128)}, f32[1,5,64,64]{3,2,1,0:T(8,128)}, u32[]{:S(2)}, u32[]{:S(2)}) collective-permute-start(f32[1,5,64,64]{3,2,1,0:T(8,128)} %get-tuple-element.17), channel_id=1, source_target_pairs={{0,1},{1,2},{2,3},{3,4},{4,5},{5,6},{6,7},{7,8},{8,9},{9,10},{10,1... | collective-permute-start | bytes 245768 | tf_op jit(solution)/shard_map/ppermute | solution.py:23
  13.7 1.9 %collective-permute-start.1 = (f32[1,5,64,64]{3,2,1,0:T(8,128)}, f32[1,5,64,64]{3,2,1,0:T(8,128)}, u32[]{:S(2)}, u32[]{:S(2)}) collective-permute-start(f32[1,5,64,64]{3,2,1,0:T(8,128)} %get-tuple-element.18), channel_id=1, source_target_pairs={{1,0},{2,1},{3,2},{4,3},{5,4},{6,5},{7,6},{8,7},{9,8},{10,9},{11,1... | collective-permute-start | bytes 245768 | tf_op jit(solution)/shard_map/ppermute | solution.py:25
  15.8 2.9 %fusion.38 = f32[480,512]{1,0:T(8,128)S(1)} fusion(f32[480,320]{1,0:T(8,128)} %constant.206.clone, f32[320,512]{1,0:T(8,128)S(1)} %bitcast.98), kind=kOutput, calls=%fused_computation.107 | convolution fusion | flops 943718400 | bytes 2252800 | tf_op jit(solution)/shard_map/dot_general | solution.py:134
  19.7 2.0 %collective-permute-start.2 = (f32[80,256]{1,0:T(8,128)S(1)}, f32[80,256]{1,0:T(8,128)S(1)}, u32[]{:S(2)}, u32[]{:S(2)}) collective-permute-start(f32[80,256]{1,0:T(8,128)S(1)} %slice.97), channel_id=1, source_target_pairs={{0,63},{1,0},{2,1},{3,2},{4,3},{5,4},{6,5},{7,6},{8,7},{9,8},{10,9... | collective-permute-start | bytes 245768 | tf_op jit(solution)/shard_map/ppermute | solution.py:35
  25.2 1.2 subtract_multiply_fusion
  29.3 1.9 %collective-permute-start.3 = (f32[80,512]{1,0:T(8,128)S(1)}, f32[80,512]{1,0:T(8,128)S(1)}, u32[]{:S(2)}, u32[]{:S(2)}) collective-permute-start(f32[80,512]{1,0:T(8,128)S(1)} %pad_maximum_fusion.1), channel_id=1, source_target_pairs={{0,63},{1,0},{2,1},{3,2},{4,3},{5,4},{6,5},{7,6},{8,7},{9,8},{10,9... | collective-permute-start | bytes 491528 | tf_op jit(solution)/shard_map/ppermute | solution.py:35
  31.3 8.6 %collective-permute-done.3 = f32[80,512]{1,0:T(8,128)S(1)} collective-permute-done((f32[80,512]{1,0:T(8,128)S(1)}, f32[80,512]{1,0:T(8,128)S(1)}, u32[]{:S(2)}, u32[]{:S(2)}) %collective-permute-start.3) | collective-permute-done | bytes 163872 | tf_op jit(solution)/shard_map/ppermute | solution.py:35
  39.9 1.9 %collective-permute-start.4 = (f32[80,512]{1,0:T(8,128)S(1)}, f32[80,512]{1,0:T(8,128)S(1)}, u32[]{:S(2)}, u32[]{:S(2)}) collective-permute-start(f32[80,512]{1,0:T(8,128)S(1)} %broadcast_select_fusion), channel_id=1, source_target_pairs={{0,62},{1,63},{2,0},{3,1},{4,2},{5,3},{6,4},{7,5},{8,6},{9,7},{10,... | collective-permute-start | bytes 491528 | tf_op jit(solution)/shard_map/ppermute | solution.py:35
  41.9 8.9 %collective-permute-done.4 = f32[80,512]{1,0:T(8,128)S(1)} collective-permute-done((f32[80,512]{1,0:T(8,128)S(1)}, f32[80,512]{1,0:T(8,128)S(1)}, u32[]{:S(2)}, u32[]{:S(2)}) %collective-permute-start.4) | collective-permute-done | bytes 163872 | tf_op jit(solution)/shard_map/ppermute | solution.py:35
  50.7 1.9 %collective-permute-start.5 = (f32[80,512]{1,0:T(8,128)S(1)}, f32[80,512]{1,0:T(8,128)S(1)}, u32[]{:S(2)}, u32[]{:S(2)}) collective-permute-start(f32[80,512]{1,0:T(8,128)S(1)} %broadcast_select_fusion.1), channel_id=1, source_target_pairs={{0,60},{1,61},{2,62},{3,63},{4,0},{5,1},{6,2},{7,3},{8,4},{9,5},{1... | collective-permute-start | bytes 491528 | tf_op jit(solution)/shard_map/ppermute | solution.py:35
  53.4 5.8 %collective-permute-done.5 = f32[80,512]{1,0:T(8,128)S(1)} collective-permute-done((f32[80,512]{1,0:T(8,128)S(1)}, f32[80,512]{1,0:T(8,128)S(1)}, u32[]{:S(2)}, u32[]{:S(2)}) %collective-permute-start.5) | collective-permute-done | bytes 163872 | tf_op jit(solution)/shard_map/ppermute | solution.py:35
  59.9 1.9 %collective-permute-start.6 = (f32[80,512]{1,0:T(8,128)}, f32[80,512]{1,0:T(8,128)}, u32[]{:S(2)}, u32[]{:S(2)}) collective-permute-start(f32[80,512]{1,0:T(8,128)} %broadcast_select_fusion.2), channel_id=1, source_target_pairs={{0,56},{1,57},{2,58},{3,59},{4,60},{5,61},{6,62},{7,63},{8,0},{9,1... | collective-permute-start | bytes 491528 | tf_op jit(solution)/shard_map/ppermute | solution.py:35
  66.1 1.4 concatenate.17
  67.5 1.4 pad_maximum_fusion
  70.4 23.1 %collective-permute-start.7 = (f32[80,512]{1,0:T(8,128)S(1)}, f32[80,512]{1,0:T(8,128)S(1)}, u32[]{:S(2)}, u32[]{:S(2)}) collective-permute-start(f32[80,512]{1,0:T(8,128)S(1)} %broadcast_select_fusion.3), channel_id=1, source_target_pairs={{0,48},{1,49},{2,50},{3,51},{4,52},{5,53},{6,54},{7,55},{8,56},{9,... | collective-permute-start | bytes 491528 | tf_op jit(solution)/shard_map/ppermute | solution.py:35
  93.5 3.3 %fusion.39 = f32[480,640]{1,0:T(8,128)} fusion(f32[480,320]{1,0:T(8,128)S(1)} %copy-done.5, f32[320,640]{1,0:T(8,128)S(1)} %bitcast.104), kind=kOutput, calls=%fused_computation.108 | convolution fusion | flops 1179648000 | bytes 2662400 | tf_op jit(solution)/shard_map/dot_general | solution.py:135
  96.9 1.8 %copy.68 = f32[6,80,640]{1,2,0:T(8,128)S(1)} copy(f32[6,80,640]{2,1,0:T(8,128)} %bitcast.100) | data formatting | bytes 2457600 | tf_op jit(solution)/shard_map/reshape | solution.py:135
  98.7 33.7 %gather_fusion.1 = f32[3072,80]{1,0:T(8,128)} fusion(f32[6,80,640]{1,2,0:T(8,128)S(1)} %copy.68, s32[3072]{0:T(1024)S(1)} %reshape.428), kind=kCustom, calls=%fused_computation.1 | custom fusion | bytes 1990656 | tf_op jit(solution)/shard_map/jit(take_along_axis)/gather | solution.py:138
  132.3 1.9 %copy.69 = f32[6,512,80]{1,2,0:T(8,128)S(1)} copy(f32[6,512,80]{2,1,0:T(8,128)} %bitcast.102) | data formatting | bytes 1966080 | tf_op jit(solution)/shard_map/jit(take_along_axis)/gather | solution.py:138
  134.2 2.1 %collective-permute-start.8 = (f32[80,512]{1,0:T(8,128)S(1)}, f32[80,512]{1,0:T(8,128)S(1)}, u32[]{:S(2)}, u32[]{:S(2)}) collective-permute-start(f32[80,512]{1,0:T(8,128)S(1)} %broadcast_select_fusion.4), channel_id=1, source_target_pairs={{0,32},{1,33},{2,34},{3,35},{4,36},{5,37},{6,38},{7,39},{8,40},{9,... | collective-permute-start | bytes 491528 | tf_op jit(solution)/shard_map/ppermute | solution.py:35
  136.5 4.9 %collective-permute-done.8 = f32[80,512]{1,0:T(8,128)S(1)} collective-permute-done((f32[80,512]{1,0:T(8,128)S(1)}, f32[80,512]{1,0:T(8,128)S(1)}, u32[]{:S(2)}, u32[]{:S(2)}) %collective-permute-start.8) | collective-permute-done | bytes 163872 | tf_op jit(solution)/shard_map/ppermute | solution.py:35
  144.2 2.3 %fusion.6 = f32[320,512]{1,0:T(8,128)S(1)} fusion(f32[320,800]{1,0:T(8,128)S(1)} %copy-done.1, f32[480,512]{1,0:T(8,128)S(1)} %bitcast.103, f32[320,512]{1,0:T(8,128)S(1)} %bitcast.99, f32[512]{0:T(512)S(1)} %copy-done.17), kind=kOutput, calls=%fused_computation.9 | convolution fusion | flops 1573437440 | bytes 3319808 | tf_op jit(solution)/shard_map/dot_general | solution.py:157
  146.5 10.0 %fusion = f32[1,5,64,512]{3,0,2,1:T(1,128)S(1)} fusion(f32[8,5,64,512]{3,2,1,0:T(8,128)} %all-gather.2.cloned.1.call-done, f32[8,8]{1,0:T(8,128)S(1)} %fusion.13, s32[]{:T(128)S(6)} %select_n.190), kind=kOutput, calls=%fused_computation.2 | convolution fusion | flops 15728640 | bytes 5898756 | tf_op jit(solution)/shard_map/ij,j...->i.../dot_general | solution.py:160
  (101 shorter events, 14.4 us)
Async XLA Ops:
  6.5 140.0 %all-gather.2.cloned.1.call-start = ((), (), s32[]{:S(2)}) async-start(), calls=%async_computation | async-start | bytes 5898240 | tf_op jit(solution)/shard_map/all_gather | solution.py:163
  7.3 14.5 %copy-start.10 = (s32[1,256]{1,0:T(1,128)S(1)}, s32[1,256]{1,0:T(1,128)}, u32[]{:S(2)}) copy-start(s32[1,256]{1,0:T(1,128)} %param.36) | copy-start | bytes 3076
  7.3 15.8 %copy-start.18 = (f32[3,5,5]{2,0,1:T(4,128)S(1)}, f32[3,5,5]{2,0,1:T(4,128)}, u32[]{:S(2)}) copy-start(f32[3,5,5]{2,0,1:T(4,128)} %param.30) | copy-start | bytes 904
  7.3 17.4 %copy-start.17 = (f32[512]{0:T(512)S(1)}, f32[512]{0:T(512)}, u32[]{:S(2)}) copy-start(f32[512]{0:T(512)} %param.29) | copy-start | bytes 6148
  7.3 17.4 %copy-start.6 = (s32[6,512]{1,0:T(8,128)S(1)}, s32[6,512]{1,0:T(8,128)}, u32[]{:S(2)}) copy-start(s32[6,512]{1,0:T(8,128)} %param.35) | copy-start | bytes 36868
  7.3 17.4 %copy-start.7 = (f32[64,64]{1,0:T(8,128)S(1)}, f32[64,64]{1,0:T(8,128)}, u32[]{:S(2)}) copy-start(f32[64,64]{1,0:T(8,128)} %constant.210.clone) | copy-start | bytes 49156
  7.3 17.4 %copy-start.8 = (f32[64,64]{1,0:T(8,128)S(1)}, f32[64,64]{1,0:T(8,128)}, u32[]{:S(2)}) copy-start(f32[64,64]{1,0:T(8,128)} %constant.209.clone) | copy-start | bytes 49156
  7.3 17.4 %copy-start.9 = (f32[64,64]{1,0:T(8,128)S(1)}, f32[64,64]{1,0:T(8,128)}, u32[]{:S(2)}) copy-start(f32[64,64]{1,0:T(8,128)} %constant.208.clone) | copy-start | bytes 49156
  9.1 58.4 %collective-permute-start = (f32[1,5,64,64]{3,2,1,0:T(8,128)}, f32[1,5,64,64]{3,2,1,0:T(8,128)}, u32[]{:S(2)}, u32[]{:S(2)}) collective-permute-start(f32[1,5,64,64]{3,2,1,0:T(8,128)} %get-tuple-element.17), channel_id=1, source_target_pairs={{0,1},{1,2},{2,3},{3,4},{4,5},{5,6},{6,7},{7,8},{8,9},{9,10},{10,1... | collective-permute-start | bytes 245768 | tf_op jit(solution)/shard_map/ppermute | solution.py:23
  13.7 53.8 %collective-permute-start.1 = (f32[1,5,64,64]{3,2,1,0:T(8,128)}, f32[1,5,64,64]{3,2,1,0:T(8,128)}, u32[]{:S(2)}, u32[]{:S(2)}) collective-permute-start(f32[1,5,64,64]{3,2,1,0:T(8,128)} %get-tuple-element.18), channel_id=1, source_target_pairs={{1,0},{2,1},{3,2},{4,3},{5,4},{6,5},{7,6},{8,7},{9,8},{10,9},{11,1... | collective-permute-start | bytes 245768 | tf_op jit(solution)/shard_map/ppermute | solution.py:25
  15.7 9.4 %copy-start.11 = (f32[64,16]{0,1:T(8,128)S(1)}, f32[64,16]{0,1:T(8,128)}, u32[]{:S(2)}) copy-start(f32[64,16]{0,1:T(8,128)} %constant.217.clone) | copy-start | bytes 12292
  15.7 9.4 %copy-start.12 = (f32[64,16]{0,1:T(8,128)S(1)}, f32[64,16]{0,1:T(8,128)}, u32[]{:S(2)}) copy-start(f32[64,16]{0,1:T(8,128)} %constant.216.clone) | copy-start | bytes 12292
  15.7 9.4 %copy-start.13 = (f32[64,16]{0,1:T(8,128)S(1)}, f32[64,16]{0,1:T(8,128)}, u32[]{:S(2)}) copy-start(f32[64,16]{0,1:T(8,128)} %constant.215.clone) | copy-start | bytes 12292
  15.7 9.4 %copy-start.14 = (f32[64,16]{0,1:T(8,128)S(1)}, f32[64,16]{0,1:T(8,128)}, u32[]{:S(2)}) copy-start(f32[64,16]{0,1:T(8,128)} %constant.214.clone) | copy-start | bytes 12292
  15.7 9.4 %copy-start.15 = (f32[64,16]{0,1:T(8,128)S(1)}, f32[64,16]{0,1:T(8,128)}, u32[]{:S(2)}) copy-start(f32[64,16]{0,1:T(8,128)} %constant.213.clone) | copy-start | bytes 12292
  15.7 9.4 %copy-start.16 = (f32[64,16]{0,1:T(8,128)S(1)}, f32[64,16]{0,1:T(8,128)}, u32[]{:S(2)}) copy-start(f32[64,16]{0,1:T(8,128)} %constant.211.clone) | copy-start | bytes 12292
  19.7 9.6 %collective-permute-start.2 = (f32[80,256]{1,0:T(8,128)S(1)}, f32[80,256]{1,0:T(8,128)S(1)}, u32[]{:S(2)}, u32[]{:S(2)}) collective-permute-start(f32[80,256]{1,0:T(8,128)S(1)} %slice.97), channel_id=1, source_target_pairs={{0,63},{1,0},{2,1},{3,2},{4,3},{5,4},{6,5},{7,6},{8,7},{9,8},{10,9... | collective-permute-start | bytes 245768 | tf_op jit(solution)/shard_map/ppermute | solution.py:35
  29.3 10.5 %collective-permute-start.3 = (f32[80,512]{1,0:T(8,128)S(1)}, f32[80,512]{1,0:T(8,128)S(1)}, u32[]{:S(2)}, u32[]{:S(2)}) collective-permute-start(f32[80,512]{1,0:T(8,128)S(1)} %pad_maximum_fusion.1), channel_id=1, source_target_pairs={{0,63},{1,0},{2,1},{3,2},{4,3},{5,4},{6,5},{7,6},{8,7},{9,8},{10,9... | collective-permute-start | bytes 491528 | tf_op jit(solution)/shard_map/ppermute | solution.py:35
  39.9 10.8 %collective-permute-start.4 = (f32[80,512]{1,0:T(8,128)S(1)}, f32[80,512]{1,0:T(8,128)S(1)}, u32[]{:S(2)}, u32[]{:S(2)}) collective-permute-start(f32[80,512]{1,0:T(8,128)S(1)} %broadcast_select_fusion), channel_id=1, source_target_pairs={{0,62},{1,63},{2,0},{3,1},{4,2},{5,3},{6,4},{7,5},{8,6},{9,7},{10,... | collective-permute-start | bytes 491528 | tf_op jit(solution)/shard_map/ppermute | solution.py:35
  50.7 8.4 %collective-permute-start.5 = (f32[80,512]{1,0:T(8,128)S(1)}, f32[80,512]{1,0:T(8,128)S(1)}, u32[]{:S(2)}, u32[]{:S(2)}) collective-permute-start(f32[80,512]{1,0:T(8,128)S(1)} %broadcast_select_fusion.1), channel_id=1, source_target_pairs={{0,60},{1,61},{2,62},{3,63},{4,0},{5,1},{6,2},{7,3},{8,4},{9,5},{1... | collective-permute-start | bytes 491528 | tf_op jit(solution)/shard_map/ppermute | solution.py:35
  59.9 9.6 %collective-permute-start.6 = (f32[80,512]{1,0:T(8,128)}, f32[80,512]{1,0:T(8,128)}, u32[]{:S(2)}, u32[]{:S(2)}) collective-permute-start(f32[80,512]{1,0:T(8,128)} %broadcast_select_fusion.2), channel_id=1, source_target_pairs={{0,56},{1,57},{2,58},{3,59},{4,60},{5,61},{6,62},{7,63},{8,0},{9,1... | collective-permute-start | bytes 491528 | tf_op jit(solution)/shard_map/ppermute | solution.py:35
  67.5 26.0 %copy-start.5 = (f32[480,320]{1,0:T(8,128)S(1)}, f32[480,320]{1,0:T(8,128)}, u32[]{:S(2)}) copy-start(f32[480,320]{1,0:T(8,128)} %constant.207.clone) | copy-start | bytes 1843204
  70.4 63.7 %collective-permute-start.7 = (f32[80,512]{1,0:T(8,128)S(1)}, f32[80,512]{1,0:T(8,128)S(1)}, u32[]{:S(2)}, u32[]{:S(2)}) collective-permute-start(f32[80,512]{1,0:T(8,128)S(1)} %broadcast_select_fusion.3), channel_id=1, source_target_pairs={{0,48},{1,49},{2,50},{3,51},{4,52},{5,53},{6,54},{7,55},{8,56},{9,... | collective-permute-start | bytes 491528 | tf_op jit(solution)/shard_map/ppermute | solution.py:35
  134.2 7.2 %collective-permute-start.8 = (f32[80,512]{1,0:T(8,128)S(1)}, f32[80,512]{1,0:T(8,128)S(1)}, u32[]{:S(2)}, u32[]{:S(2)}) collective-permute-start(f32[80,512]{1,0:T(8,128)S(1)} %broadcast_select_fusion.4), channel_id=1, source_target_pairs={{0,32},{1,33},{2,34},{3,35},{4,36},{5,37},{6,38},{7,39},{8,40},{9,... | collective-permute-start | bytes 491528 | tf_op jit(solution)/shard_map/ppermute | solution.py:35
  (6 other events, 24.7 us)
Sparse Core Ops, SparseCore 0:
  9.5 69.1 all-gather.1
where the time goes:
time: 165 us; the launch traced here: 164 us
  local copies, waits for them, and re-layouts  48 us (29%)
  starting transfers between devices  41.4 us (25%)
  waiting for transfers between devices  30.3 us (18%)
  between operations  18.9 us (11%)
  matrix products  18.4 us (11%)
  other arithmetic  7.3 us (4%)
    gather x3, local copies, waits for them, and re-layouts, shards(): jnp.take_along_axis(outer_all, neighbours[:, None, :], axis=2)  35.5 us
    ppermute x7, starting transfers between devices, shifted(): return lax.ppermute(value, axis, pairs)  34.9 us
    ppermute x7, waiting for transfers between devices, shifted(): return lax.ppermute(value, axis, pairs)  29.5 us
    dot_general x1, matrix products, shards(): jnp.einsum('ij,j...->i...', matrix_row, lax.all_gather(state, 'inst', axi...  9.96 us
    ppermute x1, starting transfers between devices, padded(): lax.ppermute(tail, axis, [(i, (i + 1) % count) for i in range(count)])  4.6 us
    dot_general x1, matrix products, shards(): jnp.dot(select_outer, flat_extended, precision=highest)  3.34 us
  transfers between devices with their start and end apart: 10, of which 6 were waited for; matrix products, arithmetic and copies ran while one was open for 37% of the time, Pallas kernels for 0%

commit v1 on v0

v1 whole, which is shorter than its diff:
```python
import functools
import math

import jax
import jax.numpy as jnp
import numpy as np
from jax import lax
from jax.experimental import pallas as pl
from jax.experimental.pallas import tpu as pltpu
from jax.sharding import PartitionSpec as P

RIM = 64
MORT = 256
ROWS = 320
ELS = 512
PIECES = 10
PIECE = ROWS // PIECES
MESH = pl.DeviceIdType.MESH
f32 = jnp.float32
bf16 = jnp.bfloat16

courant_number = 0.5


def gll_table():
    nodes = np.array([-1.0, -1.0 / math.sqrt(5.0), 1.0 / math.sqrt(5.0), 1.0])
    barycentric = np.array(
        [1.0 / np.prod([nodes[j] - nodes[k] for k in range(4) if k != j]) for j in range(4)]
    )
    derivative = np.zeros((4, 4))
    for i in range(4):
        for j in range(4):
            if i != j:
                derivative[i, j] = barycentric[j] / barycentric[i] / (nodes[i] - nodes[j])
        derivative[i, i] = -np.sum(derivative[i])
    return derivative


def node_operator():
    along = -gll_table()
    along[0, 0] -= 3.0
    along[3, 3] += 3.0
    eye = np.eye(4)
    full = np.concatenate(
        [
            np.kron(np.kron(along, eye), eye),
            np.kron(np.kron(eye, along), eye),
            np.kron(np.kron(eye, eye), along),
        ],
        axis=1,
    ).astype(np.float32)
    high = full.astype(jnp.bfloat16)
    low = (full - high.astype(np.float32)).astype(jnp.bfloat16)
    return np.concatenate([high, high, low], axis=1)


def spectral_blocks():
    count = 8

    def entry(k):
        k = k % count
        if k == 0:
            return (count * count + 2.0) / (12.0 * count)
        parity = (-1.0) ** k
        angle = math.pi * k / count
        return 0.5 * parity / math.tan(angle) + parity / (2.0 * count * math.sin(angle) ** 2)

    return [np.array([[entry(2 * d + r - s) for s in range(2)] for r in range(2)]) for d in range(4)]


def coding():
    own, near, far, back = spectral_blocks()
    turn = np.array([[0.0, -1.0], [1.0, 0.0]])

    def gap(w):
        a, b = w[:2], w[2:]
        return (near @ turn @ np.outer(a, a) - back @ turn @ np.outer(b, b) - far).ravel()

    w = np.array([0.03903, -0.69895, -1.57892, 0.64467])
    for _ in range(30):
        slope = np.stack([(gap(w + h) - gap(w - h)) / 2e-5 for h in 1e-5 * np.eye(4)], axis=1)
        w = w - np.linalg.solve(slope, gap(w))
    assert np.abs(gap(w)).max() < 1e-12
    sides = []
    for part, block, sign in ((w[:2], near, 1.0), (w[2:], back, -1.0)):
        u = part / np.linalg.norm(part)
        v = turn @ u
        sides.append((u, v, sign * float(part @ part), block @ np.linalg.inv(np.stack([u, v]))))
    table = {}
    for core, (u, v, k, mix) in enumerate(sides):
        table[core] = dict(
            mo=u[core], mp=u[1 - core], no=v[core], np=v[1 - core], k=k,
            em=mix[1 - core, 0], en=mix[1 - core, 1],
            bo=own[core, core], bp=own[core, 1 - core],
            fm=mix[core, 0], fn=mix[core, 1],
        )
    return table


def split(value):
    high = value.astype(bf16)
    low = (value - high.astype(f32)).astype(bf16)
    return high, low


def kernel(
    x_hbm, met, jac, diss, om, ang, nb, mp, dcat, out,
    X, XP, MS, MR, NS, NR, ES, ER, ACC, X4, ACC4, SA, SB, RA, RB, H,
    T, TZ, V, VU, VD, W, WU, WD, U, UX, Q, QN,
    in_sem, in4_sem, ex_s, ex_r, m_s, m_r, n_s, n_r, e_s, e_r, h_s, h_r, c_s, c_r,
):
    me = lax.axis_index("inst")
    sp = lax.axis_index("space")
    core = lax.rem(me, 2)
    mate = me + 1 - 2 * core
    ahead = lax.rem(me + 10 - 4 * core, 8)
    behind = lax.rem(me + 6 + 4 * core, 8)
    xs = lax.rem(sp, 4)
    ys = lax.rem(sp // 4, 8)
    zs = sp // 32
    nxt = lax.rem(sp + 1, 64)
    prv = lax.rem(sp + 63, 64)

    def at(z, y, x):
        return z * 32 + lax.rem(y + 8, 8) * 4 + lax.rem(x + 4, 4)

    across = at(1 - zs, ys, xs)
    y_up, y_dn = at(zs, ys + 1, xs), at(zs, ys - 1, xs)
    y_up3, y_dn3 = at(zs, ys + 3, xs), at(zs, ys - 3, xs)
    x_other = [at(zs, ys, xs + s) for s in (1, 2, 3)]

    def to(i, s):
        return {"inst": i, "space": s}

    load = pltpu.make_async_copy(x_hbm, X, in_sem)
    load.start()
    loads = [
        pltpu.make_async_copy(x_hbm.at[:, 128 * j : 128 * j + 128], X4.at[j], in4_sem.at[j]) for j in range(4)
    ]
    for copy in loads:
        copy.start()
    barrier = pltpu.get_barrier_semaphore()
    peers = [(mate, sp), (ahead, sp), (behind, sp)]
    peers += [(me, s) for s in (nxt, prv, across, y_up, y_dn, y_up3, y_dn3, *x_other)]
    for i, s in peers:
        pl.semaphore_signal(barrier, inc=1, device_id=to(i, s), device_id_type=MESH)
    pl.semaphore_wait(barrier, len(peers))
    load.wait()
    for copy in loads:
        copy.wait()

    def remote(src, dst, ss, rs, i, s):
        return pltpu.make_async_remote_copy(
            src_ref=src, dst_ref=dst, send_sem=ss, recv_sem=rs, device_id=to(i, s), device_id_type=MESH
        )

    def rows(k):
        return pl.ds(pl.multiple_of(k * PIECE, PIECE), PIECE)

    def ex(k):
        return remote(X.at[rows(k)], XP.at[rows(k)], ex_s.at[k], ex_r.at[k], mate, sp)

    def mm(k):
        return remote(MS.at[rows(k)], MR.at[rows(k)], m_s.at[k], m_r.at[k], ahead, sp)

    def nn(k):
        return remote(NS.at[rows(k)], NR.at[rows(k)], n_s.at[k], n_r.at[k], ahead, sp)

    def ee(k):
        return remote(ES.at[rows(k)], ER.at[rows(k)], e_s.at[k], e_r.at[k], mate, sp)

    table = coding()

    def coef(name):
        return jnp.where(core == 0, f32(table[0][name]), f32(table[1][name]))

    @pl.loop(0, PIECES)
    def _(k):
        ex(k).start()

    for j in range(2):
        T[:, 128 * j : 128 * j + 128] = X4[1 + j, pl.ds(0, 80, stride=4), :]
    lane = lax.broadcasted_iota(jnp.int32, (160, 128), 1)
    top, low = X[0:160, 0:128], X[160:320, 0:128]
    SA[...] = jnp.where(lane < 64, top, pltpu.roll(low, 64, 1))
    SB[...] = jnp.where(lane < 64, pltpu.roll(top, 64, 1), low)

    def stage(src, dst, slot, s):
        return remote(src, dst, c_s.at[slot], c_r.at[slot], me, s)

    hops = [
        stage(T, TZ, 0, across),
        stage(V, VD, 1, y_up), stage(V, VU, 2, y_dn),
        stage(W, WD, 3, y_up3), stage(W, WU, 4, y_dn3),
        *[stage(U, UX.at[j], 5 + j, x_other[2 - j]) for j in range(3)],
        stage(Q, QN, 8, prv),
    ]
    halo_a = remote(SA, RA, h_s.at[0], h_r.at[0], me, prv)
    halo_b = remote(SB, RB, h_s.at[1], h_r.at[1], me, nxt)

    mo, mp_ = coef("mo"), coef("mp")

    @pl.loop(0, PIECES)
    def _(k):
        ex(k).wait_recv()
        MS[rows(k)] = mo * X[rows(k)] + mp_ * XP[rows(k)]

        @pl.when(k > 0)
        def _():
            mm(jnp.maximum(k - 1, 0)).start()

        @pl.when(k == 1)
        def _():
            hops[0].start()

    halo_a.start()
    halo_b.start()
    mm(PIECES - 1).start()

    pairs = mp[...]
    rel = jnp.bitwise_and(jnp.right_shift(pairs, 8) - sp + 64, 63)
    first = rel[:, 0:1]
    below = jnp.bitwise_and(first + 63, 63)
    found = jnp.max(jnp.where(rel == below, 1, 0), axis=1, keepdims=True)
    off = jnp.where(found > 0, below, first)
    offs = jnp.broadcast_to(off, (80, MORT))
    ox = jnp.bitwise_and(offs, 3)
    oy = jnp.bitwise_and(jnp.right_shift(offs, 2), 7)
    oz = jnp.right_shift(offs, 5)
    shift = oy + jnp.where(xs < ox, 1, 0)
    flip = jnp.bitwise_and(oz + jnp.where(ys < shift, 1, 0), 1)
    short = jnp.bitwise_and(shift, 7)
    short = jnp.where(short > 4, short - 8, short)
    by3 = jnp.where(short >= 2, 1, jnp.where(short <= -2, -1, 0))
    by1 = short - 3 * by3

    hops[0].wait_recv()
    V[...] = jnp.where(flip == 1, TZ[...], T[...])

    dm = diss[0]
    node = lax.broadcasted_iota(jnp.int32, (64, ELS), 0)

    def ends(i):
        return jnp.where(jnp.bitwise_and(i + 1, 3) < 2, 1.0, 0.0)

    drag = (-3.0 * dm) * (ends(jnp.right_shift(node, 4)) + ends(jnp.right_shift(node, 2)) + ends(node))

    @pl.loop(0, 5)
    def _(g):
        highs, lows = [], []
        for d in range(3):
            mixed = jac[d, g, 0] * X[0:64]
            for h in range(1, 5):
                mixed += jac[d, g, h] * X[64 * h : 64 * h + 64]
            high, low = split(mixed)
            highs.append(high)
            lows.append(low)
        stack = jnp.concatenate(highs + lows + highs, axis=0)
        mine = pl.ds(pl.multiple_of(g * 64, 64), 64)
        ACC[mine] = jnp.dot(dcat[...], stack, preferred_element_type=f32) + drag * X[mine]

        @pl.when(g == 0)
        def _():
            hops[1].start()
            hops[2].start()

    no, np_, kk = coef("no"), coef("np"), coef("k")

    def relay(lo, hi):
        @pl.loop(lo, hi)
        def _(k):
            mm(k).wait_recv()
            NS[rows(k)] = no * X[rows(k)] + np_ * XP[rows(k)] + kk * MR[rows(k)]

            @pl.when(k > 0)
            def _():
                nn(jnp.maximum(k - 1, 0)).start()

    hops[1].wait_recv()
    hops[2].wait_recv()
    W[...] = jnp.where(by1 == 1, VU[...], jnp.where(by1 == -1, VD[...], V[...]))
    relay(0, 3)
    hops[3].start()
    hops[4].start()

    halo_a.wait_recv()
    halo_b.wait_recv()
    H[0:160] = jnp.where(lane < 64, RB[...], pltpu.roll(RA[...], 64, 1))
    H[160:320] = jnp.where(lane < 64, pltpu.roll(RB[...], 64, 1), RA[...])

    ACC4[...] = jnp.zeros_like(ACC4)
    column = lax.broadcasted_iota(jnp.int32, (640, ELS), 0)

    def mix(face, outer, g):
        d, sign = face // 2, (1.0 if face % 2 else -1.0)
        total = (3.0 * dm) * outer[g]
        for h in range(5):
            total -= (3.0 * sign) * jac[d, g, h] * outer[h]
        return total

    def gather_face(face):
        d, end = face // 2, 3 * (face % 2)
        far = 3 - end

        def pick(ref):
            if d == 0:
                return jnp.concatenate([ref[64 * g + 16 * far : 64 * g + 16 * far + 16] for g in range(5)], axis=0)
            if d == 1:
                t = 8 * (far // 2)
                return jnp.concatenate([ref[16 * a + t : 16 * a + t + 8] for a in range(20)], axis=0)

        if d == 2:
            picked = [X4[j, pl.ds(far, 80, stride=4), :] for j in range(4)] + [H[pl.ds(far, 80, stride=4), :]]
        else:
            picked = [pick(X), pick(H)]
        source = jnp.concatenate(picked, axis=1)
        high, low = split(source)
        k = nb[face : face + 1, :]
        place = jnp.where(k < RIM, k + ELS, jnp.where(k < RIM + ELS, k - RIM, k))
        if face == 5:
            q = lax.broadcasted_iota(jnp.int32, (1, ELS), 1)
            place = jnp.where((q >= 2 * RIM) & (q < 2 * RIM + MORT), -1, place)
        hot = jnp.where(column == place, 1.0, 0.0).astype(bf16)
        both = jnp.dot(jnp.concatenate([high, low], axis=0), hot, preferred_element_type=f32)
        count = source.shape[0]
        got = both[:count] + both[count:]
        per = count // 5
        outer = [got[per * h : per * h + per] for h in range(5)]
        for g in range(5):
            part = mix(face, outer, g)
            if d == 0:
                ACC[64 * g + 16 * end : 64 * g + 16 * end + 16] += part
            elif d == 1:
                sub = lax.broadcasted_iota(jnp.int32, (8, ELS), 0)
                t = 8 * (end // 2)
                keep = (sub >= 4) if end == 3 else (sub < 4)
                for a in range(4):
                    piece = pltpu.roll(part[8 * a : 8 * a + 8], 4, 0)
                    at_row = 64 * g + 16 * a + t
                    ACC[at_row : at_row + 8] += jnp.where(keep, piece, 0.0)
            else:
                for j in range(4):
                    ACC4[j, pl.ds(64 * g + end, 16, stride=4), :] = part[:, 128 * j : 128 * j + 128]

    gather_face(0)
    relay(3, 6)
    gather_face(1)
    hops[3].wait_recv()
    hops[4].wait_recv()
    U[...] = jnp.where(by3 == 1, WU[...], jnp.where(by3 == -1, WD[...], W[...]))
    gather_face(2)
    for j in range(3):
        hops[5 + j].start()
    relay(6, PIECES)
    gather_face(3)
    nn(PIECES - 1).start()
    for j in range(3):
        hops[5 + j].wait_recv()
    Q[...] = jnp.where(ox == 0, U[...], jnp.where(ox == 1, UX[0], jnp.where(ox == 2, UX[1], UX[2])))
    gather_face(4)
    hops[8].start()
    gather_face(5)

    hops[8].wait_recv()
    window = jnp.concatenate([Q[...], QN[...]], axis=1)
    high, low = split(window)
    index = jnp.bitwise_and(rel - off + 64, 63) * MORT + jnp.bitwise_and(pairs, MORT - 1)
    hot = jnp.where(lax.broadcasted_iota(jnp.int32, (2 * MORT, MORT), 0) == index, 1.0, 0.0).astype(bf16)
    both = jnp.dot(jnp.concatenate([high, low], axis=0), hot, preferred_element_type=f32)
    got = both[:80] + both[80:]
    outer = [got[16 * h : 16 * h + 16] for h in range(5)]
    turn = jnp.full((16, MORT), ang[0], f32)
    cosine, sine = jnp.cos(turn), jnp.sin(turn)
    outer[2], outer[3] = cosine * outer[2] - sine * outer[3], sine * outer[2] + cosine * outer[3]
    for g in range(5):
        part = mix(5, outer, g)
        for j in range(2):
            ACC4[1 + j, pl.ds(64 * g + 3, 16, stride=4), :] += part[:, 128 * j : 128 * j + 128]

    metric = met[...]
    w0 = om[0]
    pace = courant_number / (metric * dm + w0)
    gain = pace * metric
    drop = pace * w0
    bo, bp, fm, fn, em, en = [coef(c) for c in ("bo", "bp", "fm", "fn", "em", "en")]

    @pl.loop(0, PIECES)
    def _(k):
        r = rows(k)
        face = jnp.concatenate([ACC4[j, r] for j in range(4)], axis=1)
        ACC[r] = X[r] + gain * (ACC[r] + face) - drop * (bo * X[r] + bp * XP[r] + fm * MR[r])

    def finish(k):
        ee(k).wait_recv()
        r = rows(k)
        out[r] = ACC[r] - drop * (fn * NR[r] + ER[r])

    @pl.loop(0, PIECES)
    def _(k):
        nn(k).wait_recv()
        r = rows(k)
        ES[r] = em * MR[r] + en * NR[r]

        @pl.when(k > 0)
        def _():
            finish(jnp.maximum(k - 1, 0))

        ee(k).start()

    finish(PIECES - 1)

    @pl.loop(0, PIECES)
    def _(k):
        for copy in (ex, mm, nn, ee):
            copy(k).wait_send()

    for copy in (*hops, halo_a, halo_b):
        copy.wait_send()


def shards(state, metric, jacobians, dissipation, omega, rotor_angle, counts, neighbours, mortar_pairs):
    vmem = pl.BlockSpec(memory_space=pltpu.VMEM)
    smem = pl.BlockSpec(memory_space=pltpu.SMEM)
    whole = pltpu.VMEM((ROWS, ELS), f32)
    half = pltpu.VMEM((160, 128), f32)
    trace = pltpu.VMEM((80, MORT), f32)
    sem = pltpu.SemaphoreType.DMA
    result = pl.pallas_call(
        kernel,
        out_shape=jax.ShapeDtypeStruct((ROWS, ELS), f32),
        in_specs=[pl.BlockSpec(memory_space=pl.ANY), vmem, smem, smem, smem, smem, vmem, vmem, vmem],
        out_specs=vmem,
        scratch_shapes=[whole] * 9
        + [pltpu.VMEM((4, ROWS, 128), f32)] * 2
        + [half] * 4
        + [pltpu.VMEM((ROWS, 128), f32)]
        + [trace] * 9
        + [pltpu.VMEM((3, 80, MORT), f32)]
        + [trace] * 2
        + [sem(()), sem((4,))]
        + [sem((PIECES,))] * 8
        + [sem((2,))] * 2
        + [sem((9,))] * 2,
        compiler_params=pltpu.CompilerParams(collective_id=0, has_side_effects=True),
        name="step",
    )(
        state.reshape(ROWS, ELS),
        metric.reshape(1, ELS),
        jacobians,
        dissipation,
        omega,
        rotor_angle,
        neighbours,
        mortar_pairs,
        jnp.asarray(node_operator()),
    )
    live = jnp.arange(ELS, dtype=jnp.int32) < counts[0]
    return jnp.where(live, result.reshape(state.shape), jnp.float32(0.0))


def solution(mesh):
    return jax.shard_map(
        shards,
        mesh=mesh,
        in_specs=(
            P("inst", None, None, "space"),
            P("space"),
            P(),
            P(),
            P(),
            P("inst"),
            P("space"),
            P(None, "space"),
            P("inst", "space"),
        ),
        out_specs=P("inst", None, None, "space"),
        check_vma=False,
    )
```

time: 165 us -> 67.9 us (0.41)
  the two profiles are of different devices: /device:TPU:30 before, /device:TPU:1 now
where the time goes in v1:
time: 67.9 us; the launch traced here: 67.7 us
  Pallas kernels  62.4 us (92%)
  between operations  2.63 us (4%)
  other arithmetic  2 us (3%)
    pallas_call x1, Pallas kernels, shards(): pl.pallas_call(kernel, out_shape=jax.ShapeDtypeStruct((ROWS, ELS), f32),...  62.4 us
    select_n x1, other arithmetic, shards(): return jnp.where(live, result.reshape(state.shape), jnp.float32(0.0))  1.99 us

profile of v1, /device:TPU:1, one launch (start us, length us, event | category | flops | bytes accessed | tf_op | source)
XLA Modules:
  0.0 67.7 jit_solution(15317716170143647050)
XLA Ops:
  0.0 0.0 copy-start
  2.6 0.0 copy-done
  2.6 0.6 copy.11.jac
  3.2 62.4 %step.1 = f32[320,512]{1,0:T(8,128)} custom-call(f32[320,512]{1,0:T(8,128)} %bitcast.6, f32[1,512]{1,0:T(1,128)} %bitcast.7, f32[3,5,5]{2,1,0:T(8,128)} %copy.11.jac, f32[1]{0:T(128)S(6)} %copy.12.diss, f32[1]{0:T(128)S(6)} %copy.13.om, f32[1]{0:T(128)S(6)} %copy.14.ang, s32[6,512]{1,0:T(8,128)} %nb.1, s32[1,256]{1,0:T(1,128)} %mp.1, ...), custom_call_target="tpu_custom_call" | custom-call | tf_op jit(solution)/shard_map/step/pallas_call | solution.py:428
  65.7 2.0 %broadcast_select_fusion = f32[1,5,64,512]{3,2,1,0:T(8,128)} fusion(f32[1,5,64,512]{3,2,1,0:T(8,128)} %bitcast.5, pred[512]{0:T(512)(128)(4,1)S(1)} %iota_compare_fusion), kind=kLoop, calls=%fused_computation | loop fusion | flops 163840 | bytes 1311232 | tf_op jit(solution)/shard_map/jit(_where)/select_n | solution.py:458
  (1 shorter events, 0.0 us)
Async XLA Ops:
  0.0 2.6 %copy-start = (f32[3,5,5]{2,0,1:T(4,128)S(1)}, f32[3,5,5]{2,0,1:T(4,128)}, u32[]{:S(2)}) copy-start(f32[3,5,5]{2,0,1:T(4,128)} %param.12) | copy-start | bytes 904

commit v2 on v1

v2 whole, which is shorter than its diff:
```python
import functools
import math

import jax
import jax.numpy as jnp
import numpy as np
from jax import lax
from jax.experimental import pallas as pl
from jax.experimental.pallas import tpu as pltpu
from jax.sharding import PartitionSpec as P

RIM = 64
MORT = 256
ROWS = 320
ELS = 512
STEPS = 5
PIECE = ROWS // 2 // STEPS
VMEM_BYTES = 24 * 2**20
MESH = pl.DeviceIdType.MESH
f32 = jnp.float32
bf16 = jnp.bfloat16

courant_number = 0.5


def gll_table():
    nodes = np.array([-1.0, -1.0 / math.sqrt(5.0), 1.0 / math.sqrt(5.0), 1.0])
    barycentric = np.array(
        [1.0 / np.prod([nodes[j] - nodes[k] for k in range(4) if k != j]) for j in range(4)]
    )
    derivative = np.zeros((4, 4))
    for i in range(4):
        for j in range(4):
            if i != j:
                derivative[i, j] = barycentric[j] / barycentric[i] / (nodes[i] - nodes[j])
        derivative[i, i] = -np.sum(derivative[i])
    return derivative


def node_operator():
    along = -gll_table()
    along[0, 0] -= 3.0
    along[3, 3] += 3.0
    eye = np.eye(4)
    full = np.concatenate(
        [
            np.kron(np.kron(along, eye), eye),
            np.kron(np.kron(eye, along), eye),
            np.kron(np.kron(eye, eye), along),
        ],
        axis=1,
    ).astype(np.float32)
    high = full.astype(jnp.bfloat16)
    low = (full - high.astype(np.float32)).astype(jnp.bfloat16)
    return np.concatenate([high, high, low], axis=1)


def spectral_blocks():
    count = 8

    def entry(k):
        k = k % count
        if k == 0:
            return (count * count + 2.0) / (12.0 * count)
        parity = (-1.0) ** k
        angle = math.pi * k / count
        return 0.5 * parity / math.tan(angle) + parity / (2.0 * count * math.sin(angle) ** 2)

    return [np.array([[entry(2 * d + r - s) for s in range(2)] for r in range(2)]) for d in range(4)]


def coding():
    own, near, far, back = spectral_blocks()
    turn = np.array([[0.0, -1.0], [1.0, 0.0]])

    def gap(w):
        a, b = w[:2], w[2:]
        return (near @ turn @ np.outer(a, a) - back @ turn @ np.outer(b, b) - far).ravel()

    w = np.array([0.03903, -0.69895, -1.57892, 0.64467])
    for _ in range(30):
        slope = np.stack([(gap(w + h) - gap(w - h)) / 2e-5 for h in 1e-5 * np.eye(4)], axis=1)
        w = w - np.linalg.solve(slope, gap(w))
    assert np.abs(gap(w)).max() < 1e-12
    sides = []
    for part, block, sign in ((w[:2], near, 1.0), (w[2:], back, -1.0)):
        u = part / np.linalg.norm(part)
        v = turn @ u
        sides.append((u, v, sign * float(part @ part), block @ np.linalg.inv(np.stack([u, v]))))
    table = [[], []]
    for side, (u, v, k, mix) in enumerate(sides):
        for core in range(2):
            table[side].append(dict(
                mo=u[core], mp=u[1 - core], no=v[core], np=v[1 - core], k=k,
                em=mix[1 - core, 0], en=mix[1 - core, 1],
                bo=own[core, core], bp=own[core, 1 - core],
                fm=mix[core, 0], fn=mix[core, 1],
            ))
    return table


def split(value):
    high = value.astype(bf16)
    low = (value - high.astype(f32)).astype(bf16)
    return high, low


def kernel(
    x_hbm, met_hbm, jac_hbm, diss_hbm, om_hbm, ang_hbm, cnt_hbm, nb_hbm, mp_hbm, dcat_hbm, out,
    X, XP, MS, MR, NS, NR, ES, ER, ACC, X4, ACC4, SA, SB, RA, RB, H,
    T, TZ, V, VU, VD, W, WU, WD, U, UX, Q, QN,
    met, nb, mp, dcat, jac, diss, om, ang, cnt,
    in_sem, ex_s, ex_r, m_s, m_r, n_s, n_r, e_s, e_r, h_s, h_r, c_s, c_r,
):
    me = lax.axis_index("inst")
    sp = lax.axis_index("space")
    core = lax.rem(me, 2)
    mate = me + 1 - 2 * core
    up = lax.rem(me + 2, 8)
    down = lax.rem(me + 6, 8)
    xs = lax.rem(sp, 4)
    ys = lax.rem(sp // 4, 8)
    zs = sp // 32
    nxt = lax.rem(sp + 1, 64)
    prv = lax.rem(sp + 63, 64)

    def at(z, y, x):
        return z * 32 + lax.rem(y + 8, 8) * 4 + lax.rem(x + 4, 4)

    across = at(1 - zs, ys, xs)
    y_up, y_dn = at(zs, ys + 1, xs), at(zs, ys - 1, xs)
    y_up3, y_dn3 = at(zs, ys + 3, xs), at(zs, ys - 3, xs)
    x_other = [at(zs, ys, xs + s) for s in (1, 2, 3)]

    def to(i, s):
        return {"inst": i, "space": s}

    barrier = pltpu.get_barrier_semaphore()
    peers = [(mate, sp), (up, sp), (down, sp)]
    peers += [(me, s) for s in (nxt, prv, across, y_up, y_dn, y_up3, y_dn3, *x_other)]
    for i, s in peers:
        pl.semaphore_signal(barrier, inc=1, device_id=to(i, s), device_id_type=MESH)
    pairs_in = [(x_hbm, X)]
    pairs_in += [(x_hbm.at[:, 128 * j : 128 * j + 128], X4.at[j]) for j in range(4)]
    pairs_in += [
        (jac_hbm, jac), (diss_hbm, diss), (mp_hbm, mp), (dcat_hbm, dcat), (nb_hbm, nb),
        (om_hbm, om), (ang_hbm, ang), (cnt_hbm, cnt), (met_hbm, met),
    ]
    loads = [pltpu.make_async_copy(a, b, in_sem.at[j]) for j, (a, b) in enumerate(pairs_in)]
    for copy in loads:
        copy.start()
    for copy in loads:
        copy.wait()

    for j in range(2):
        T[:, 128 * j : 128 * j + 128] = X4[1 + j, pl.ds(0, 80, stride=4), :]
    lane = lax.broadcasted_iota(jnp.int32, (160, 128), 1)
    top, low = X[0:160, 0:128], X[160:320, 0:128]
    SA[...] = jnp.where(lane < 64, top, pltpu.roll(low, 64, 1))
    SB[...] = jnp.where(lane < 64, pltpu.roll(top, 64, 1), low)

    def remote(src, dst, ss, rs, i, s):
        return pltpu.make_async_remote_copy(
            src_ref=src, dst_ref=dst, send_sem=ss, recv_sem=rs, device_id=to(i, s), device_id_type=MESH
        )

    def half(side):
        return jnp.bitwise_xor(core, side) * (ROWS // 2)

    def rows(side, k):
        return pl.ds(pl.multiple_of(half(side) + k * PIECE, PIECE), PIECE)

    def flow(a, b, ss, rs, device):
        def piece(side, k):
            r = rows(side, k)
            target = mate if device is None else device[side]
            return remote(a.at[r], b.at[r], ss.at[side], rs.at[side, k], target, sp)

        def all_sent(side):
            r = pl.ds(pl.multiple_of(half(side), PIECE), ROWS // 2)
            target = mate if device is None else device[side]
            return remote(a.at[r], b.at[r], ss.at[side], rs.at[side, 0], target, sp)

        return piece, all_sent

    def plain(k, h):
        return pl.ds(pl.multiple_of(h * (ROWS // 2) + k * PIECE, PIECE), PIECE)

    def ex(h, k):
        r = plain(k, h)
        return remote(X.at[r], XP.at[r], ex_s, ex_r.at[h, k], mate, sp)

    mm, mm_sent = flow(MS, MR, m_s, m_r, (up, down))
    nn, nn_sent = flow(NS, NR, n_s, n_r, (up, down))
    ee, ee_sent = flow(ES, ER, e_s, e_r, None)

    def stage(src, dst, slot, s):
        return remote(src, dst, c_s.at[slot], c_r.at[slot], me, s)

    hops = [
        stage(T, TZ, 0, across),
        stage(V, VD, 1, y_up), stage(V, VU, 2, y_dn),
        stage(W, WD, 3, y_up3), stage(W, WU, 4, y_dn3),
        *[stage(U, UX.at[j], 5 + j, x_other[2 - j]) for j in range(3)],
        stage(Q, QN, 8, prv),
    ]
    halo_a = remote(SA, RA, h_s.at[0], h_r.at[0], me, prv)
    halo_b = remote(SB, RB, h_s.at[1], h_r.at[1], me, nxt)

    pl.semaphore_wait(barrier, len(peers))
    hops[0].start()

    @pl.loop(0, STEPS)
    def _(k):
        for h in range(2):
            ex(h, k).start()

    table = coding()

    def coef(name, side):
        return jnp.where(core == 0, f32(table[side][0][name]), f32(table[side][1][name]))

    def combine(names, parts, side, r):
        total = coef(names[0], side) * parts[0][r]
        for name, ref in zip(names[1:], parts[1:]):
            total += coef(name, side) * ref[r]
        return total

    @pl.loop(0, STEPS)
    def _(k):
        for h in range(2):
            ex(h, k).wait_recv()
        for side in range(2):
            r = rows(side, k)
            MS[r] = combine(("mo", "mp"), (X, XP), side, r)

        @pl.when(k > 0)
        def _():
            for side in range(2):
                mm(side, jnp.maximum(k - 1, 0)).start()

    halo_a.start()
    halo_b.start()
    for side in range(2):
        mm(side, STEPS - 1).start()

    pairs = mp[...]
    rel = jnp.bitwise_and(jnp.right_shift(pairs, 8) - sp + 64, 63)
    first = rel[:, 0:1]
    below = jnp.bitwise_and(first + 63, 63)
    found = jnp.max(jnp.where(rel == below, 1, 0), axis=1, keepdims=True)
    off = jnp.where(found > 0, below, first)
    offs = jnp.broadcast_to(off, (80, MORT))
    ox = jnp.bitwise_and(offs, 3)
    oy = jnp.bitwise_and(jnp.right_shift(offs, 2), 7)
    oz = jnp.right_shift(offs, 5)
    shift = oy + jnp.where(xs < ox, 1, 0)
    flip = jnp.bitwise_and(oz + jnp.where(ys < shift, 1, 0), 1)
    short = jnp.bitwise_and(shift, 7)
    short = jnp.where(short > 4, short - 8, short)
    by3 = jnp.where(short >= 2, 1, jnp.where(short <= -2, -1, 0))
    by1 = short - 3 * by3

    dm = diss[0, 0]
    node = lax.broadcasted_iota(jnp.int32, (64, ELS), 0)

    def ends(i):
        return jnp.where(jnp.bitwise_and(i + 1, 3) < 2, 1.0, 0.0)

    drag = (-3.0 * dm) * (ends(jnp.right_shift(node, 4)) + ends(jnp.right_shift(node, 2)) + ends(node))

    @pl.loop(0, 5)
    def _(g):
        highs, lows = [], []
        for d in range(3):
            mixed = jac[g, d, 0] * X[0:64]
            for h in range(1, 5):
                mixed += jac[g, d, h] * X[64 * h : 64 * h + 64]
            high, low = split(mixed)
            highs.append(high)
            lows.append(low)
        stack = jnp.concatenate(highs + lows + highs, axis=0)
        mine = pl.ds(pl.multiple_of(g * 64, 64), 64)
        ACC[mine] = jnp.dot(dcat[...], stack, preferred_element_type=f32) + drag * X[mine]

    def relay(first_step, last_step):
        @pl.loop(first_step, last_step)
        def _(k):
            for side in range(2):
                mm(side, k).wait_recv()
                r = rows(side, k)
                NS[r] = combine(("no", "np", "k"), (X, XP, MR), side, r)

            @pl.when(k > 0)
            def _():
                for side in range(2):
                    nn(side, jnp.maximum(k - 1, 0)).start()

    hops[0].wait_recv()
    V[...] = jnp.where(flip == 1, TZ[...], T[...])
    ACC4[...] = jnp.zeros_like(ACC4)
    hops[1].start()
    hops[2].start()

    column = lax.broadcasted_iota(jnp.int32, (640, ELS), 0)

    def mix(face, outer, g):
        d, sign = face // 2, (1.0 if face % 2 else -1.0)
        total = (3.0 * dm) * outer[g]
        for h in range(5):
            total -= (3.0 * sign) * jac[g, d, h] * outer[h]
        return total

    def gather_face(face):
        d, end = face // 2, 3 * (face % 2)
        far = 3 - end

        def pick(ref):
            if d == 0:
                return jnp.concatenate([ref[64 * g + 16 * far : 64 * g + 16 * far + 16] for g in range(5)], axis=0)
            t = 8 * (far // 2)
            return jnp.concatenate([ref[16 * a + t : 16 * a + t + 8] for a in range(20)], axis=0)

        if d == 2:
            picked = [X4[j, pl.ds(far, 80, stride=4), :] for j in range(4)] + [H[pl.ds(far, 80, stride=4), :]]
        else:
            picked = [pick(X), pick(H)]
        source = jnp.concatenate(picked, axis=1)
        high, low = split(source)
        k = nb[face : face + 1, :]
        place = jnp.where(k < RIM, k + ELS, jnp.where(k < RIM + ELS, k - RIM, k))
        if face == 5:
            q = lax.broadcasted_iota(jnp.int32, (1, ELS), 1)
            place = jnp.where((q >= 2 * RIM) & (q < 2 * RIM + MORT), -1, place)
        hot = jnp.where(column == place, 1.0, 0.0).astype(bf16)
        both = jnp.dot(jnp.concatenate([high, low], axis=0), hot, preferred_element_type=f32)
        count = source.shape[0]
        got = both[:count] + both[count:]
        per = count // 5
        outer = [got[per * h : per * h + per] for h in range(5)]
        for g in range(5):
            part = mix(face, outer, g)
            if d == 0:
                ACC[64 * g + 16 * end : 64 * g + 16 * end + 16] += part
            elif d == 1:
                sub = lax.broadcasted_iota(jnp.int32, (8, ELS), 0)
                t = 8 * (end // 2)
                keep = (sub >= 4) if end == 3 else (sub < 4)
                for a in range(4):
                    piece = pltpu.roll(part[8 * a : 8 * a + 8], 4, 0)
                    at_row = 64 * g + 16 * a + t
                    ACC[at_row : at_row + 8] += jnp.where(keep, piece, 0.0)
            else:
                for j in range(4):
                    ACC4[j, pl.ds(64 * g + end, 16, stride=4), :] = part[:, 128 * j : 128 * j + 128]

    relay(0, 1)
    halo_a.wait_recv()
    halo_b.wait_recv()
    H[0:160] = jnp.where(lane < 64, RB[...], pltpu.roll(RA[...], 64, 1))
    H[160:320] = jnp.where(lane < 64, pltpu.roll(RB[...], 64, 1), RA[...])
    gather_face(0)
    gather_face(1)
    hops[1].wait_recv()
    hops[2].wait_recv()
    W[...] = jnp.where(by1 == 1, VU[...], jnp.where(by1 == -1, VD[...], V[...]))
    gather_face(2)
    hops[3].start()
    hops[4].start()
    gather_face(3)
    relay(1, STEPS)
    gather_face(4)
    for side in range(2):
        nn(side, STEPS - 1).start()
    gather_face(5)
    hops[3].wait_recv()
    hops[4].wait_recv()
    U[...] = jnp.where(by3 == 1, WU[...], jnp.where(by3 == -1, WD[...], W[...]))

    metric = met[...]
    w0 = om[0, 0]
    pace = courant_number / (metric * dm + w0)
    gain = pace * metric
    drop = pace * w0
    live = lax.broadcasted_iota(jnp.int32, (1, ELS), 1) < cnt[0, 0]
    gain = jnp.where(live, gain, 0.0)
    drop = jnp.where(live, drop, 0.0)
    keep = jnp.where(live, 1.0, 0.0)
    for j in range(3):
        hops[5 + j].start()
    remote(X, XP, ex_s, ex_r.at[0, 0], mate, sp).wait_send()
    for side in range(2):
        mm_sent(side).wait_send()
    for j in range(3):
        hops[5 + j].wait_recv()
    Q[...] = jnp.where(ox == 0, U[...], jnp.where(ox == 1, UX[0], jnp.where(ox == 2, UX[1], UX[2])))
    turn = jnp.full((16, MORT), ang[0, 0], f32)
    cosine, sine = jnp.cos(turn), jnp.sin(turn)
    index = jnp.bitwise_and(rel - off + 64, 63) * MORT + jnp.bitwise_and(pairs, MORT - 1)
    hot = jnp.where(lax.broadcasted_iota(jnp.int32, (2 * MORT, MORT), 0) == index, 1.0, 0.0).astype(bf16)
    hops[8].start()
    for copy in (*hops[:8], halo_a, halo_b):
        copy.wait_send()

    hops[8].wait_recv()
    window = jnp.concatenate([Q[...], QN[...]], axis=1)
    high, low = split(window)
    both = jnp.dot(jnp.concatenate([high, low], axis=0), hot, preferred_element_type=f32)
    got = both[:80] + both[80:]
    outer = [got[16 * h : 16 * h + 16] for h in range(5)]
    outer[2], outer[3] = cosine * outer[2] - sine * outer[3], sine * outer[2] + cosine * outer[3]
    for g in range(5):
        part = mix(5, outer, g)
        for j in range(2):
            ACC4[1 + j, pl.ds(64 * g + 3, 16, stride=4), :] += part[:, 128 * j : 128 * j + 128]

    @pl.loop(0, STEPS)
    def _(k):
        for side in range(2):
            r = rows(side, k)
            face = jnp.concatenate([ACC4[j, r] for j in range(4)], axis=1)
            ACC[r] = keep * X[r] + gain * (ACC[r] + face) - drop * combine(("bo", "bp", "fm"), (X, XP, MR), side, r)

    def finish(k):
        for side in range(2):
            ee(1 - side, k).wait_recv()
            r = rows(side, k)
            out[r] = ACC[r] - drop * (coef("fn", side) * NR[r] + ER[r])

    @pl.loop(0, STEPS)
    def _(k):
        for side in range(2):
            nn(side, k).wait_recv()
            r = rows(side, k)
            ES[r] = combine(("em", "en"), (MR, NR), side, r)

        @pl.when(k > 0)
        def _():
            finish(jnp.maximum(k - 1, 0))

        for side in range(2):
            ee(side, k).start()

    hops[8].wait_send()
    for side in range(2):
        nn_sent(side).wait_send()
    finish(STEPS - 1)
    for side in range(2):
        ee_sent(side).wait_send()


def shards(state, metric, jacobians, dissipation, omega, rotor_angle, counts, neighbours, mortar_pairs):
    anywhere = pl.BlockSpec(memory_space=pltpu.HBM)
    whole = pltpu.VMEM((ROWS, ELS), f32)
    quarter = pltpu.VMEM((160, 128), f32)
    trace = pltpu.VMEM((80, MORT), f32)
    sem = pltpu.SemaphoreType.DMA
    operands = [
        state.reshape(ROWS, ELS),
        metric.reshape(1, ELS),
        jnp.transpose(jacobians, (1, 0, 2)),
        dissipation.reshape(1, 1),
        omega.reshape(1, 1),
        rotor_angle.reshape(1, 1),
        counts.reshape(1, 1),
        neighbours,
        mortar_pairs,
        jnp.asarray(node_operator()),
    ]
    operands = [a if a.size == 1 else pltpu.with_memory_space_constraint(a, pltpu.HBM) for a in operands]
    result = pl.pallas_call(
        kernel,
        out_shape=jax.ShapeDtypeStruct((ROWS, ELS), f32),
        in_specs=[pl.BlockSpec(memory_space=pltpu.VMEM) if a.size == 1 else anywhere for a in operands],
        out_specs=pl.BlockSpec(memory_space=pltpu.VMEM),
        scratch_shapes=[whole] * 9
        + [pltpu.VMEM((4, ROWS, 128), f32)] * 2
        + [quarter] * 4
        + [pltpu.VMEM((ROWS, 128), f32)]
        + [trace] * 9
        + [pltpu.VMEM((3, 80, MORT), f32)]
        + [trace] * 2
        + [pltpu.VMEM((1, ELS), f32), pltpu.VMEM((6, ELS), jnp.int32), pltpu.VMEM((1, MORT), jnp.int32)]
        + [pltpu.VMEM((64, 576), bf16), pltpu.SMEM((5, 3, 5), f32)]
        + [pltpu.SMEM((1, 1), f32)] * 3
        + [pltpu.SMEM((1, 1), jnp.int32)]
        + [sem((14,)), sem(()), sem((2, STEPS))]
        + [sem((2,)), sem((2, STEPS))] * 3
        + [sem((2,))] * 2
        + [sem((9,))] * 2,
        compiler_params=pltpu.CompilerParams(collective_id=0, has_side_effects=True, vmem_limit_bytes=VMEM_BYTES),
        name="step",
    )(
        *operands,
    )
    return result.reshape(state.shape)


def solution(mesh):
    return jax.shard_map(
        shards,
        mesh=mesh,
        in_specs=(
            P("inst", None, None, "space"),
            P("space"),
            P(),
            P(),
            P(),
            P("inst"),
            P("space"),
            P(None, "space"),
            P("inst", "space"),
        ),
        out_specs=P("inst", None, None, "space"),
        check_vma=False,
    )
```

time: 67.9 us -> 60.7 us (0.89)
  Pallas kernels: 62.4 us -> 57.1 us
  other arithmetic: 2 us -> 0 us
    pallas_call x1, Pallas kernels: 62.4 us -> 57.1 us  [shards(): pl.pallas_call(kernel, out_shape=jax.ShapeDtypeStruct((ROWS, ELS), f32),...]
    select_n x1 -> x0, other arithmetic: 1.99 us -> none  [shards(): return jnp.where(live, result.reshape(state.shape), jnp.float32(0.0))]
where the time goes in v2:
time: 60.7 us; the launch traced here: 60.5 us
  Pallas kernels  57.1 us (94%)
  between operations  2.59 us (4%)
  local copies, waits for them, and re-layouts  0.84 us (1%)
    pallas_call x1, Pallas kernels, shards(): pl.pallas_call(kernel, out_shape=jax.ShapeDtypeStruct((ROWS, ELS), f32),...  57.1 us

profile of v2, /device:TPU:1, one launch (start us, length us, event | category | flops | bytes accessed | tf_op | source)
XLA Modules:
  0.0 60.5 jit_solution(1719323187586408161)
XLA Ops:
  2.6 57.1 %step.1 = f32[320,512]{1,0:T(8,128)S(1)} custom-call(f32[320,512]{1,0:T(8,128)} %bitcast.13, f32[1,512]{1,0:T(1,128)} %bitcast.15, f32[5,3,5]{2,1,0:T(4,128)} %bitcast.14, f32[1,1]{1,0:T(1,128)} %bitcast.8.diss_hbm, f32[1,1]{1,0:T(1,128)} %bitcast.9.om_hbm, f32[1,1]{1,0:T(1,128)} %bitcast.10.ang_hbm, s32[1,1]{1,0:T(1,128)} %bitcast.11.cnt_hbm, ...), custom_call_target="tpu_custom_call" | custom-call | tf_op jit(solution)/shard_map/step/pallas_call | solution.py:471
  59.7 0.8 %copy.16 = f32[1,5,64,512]{3,2,1,0:T(8,128)} copy(f32[1,5,64,512]{3,2,1,0:T(8,128)S(1)} %bitcast.12) | data formatting | bytes 1310720

commit v3 on v2

--- a/solution.py
+++ b/solution.py
@@ -107,10 +107,10 @@
 
 def kernel(
     x_hbm, met_hbm, jac_hbm, diss_hbm, om_hbm, ang_hbm, cnt_hbm, nb_hbm, mp_hbm, dcat_hbm, out,
-    X, XP, MS, MR, NS, NR, ES, ER, ACC, X4, ACC4, SA, SB, RA, RB, H,
+    X, XP, MS, MR, NS, NR, ES, ER, ACC, OUT, X4, ACC4, SA, SB, RA, RB, H,
     T, TZ, V, VU, VD, W, WU, WD, U, UX, Q, QN,
     met, nb, mp, dcat, jac, diss, om, ang, cnt,
-    in_sem, ex_s, ex_r, m_s, m_r, n_s, n_r, e_s, e_r, h_s, h_r, c_s, c_r,
+    in_sem, ex_s, ex_r, m_s, m_r, n_s, n_r, e_s, e_r, h_s, h_r, c_s, c_r, out_sem,
 ):
     me = lax.axis_index("inst")
     sp = lax.axis_index("space")
@@ -140,8 +140,9 @@
     peers += [(me, s) for s in (nxt, prv, across, y_up, y_dn, y_up3, y_dn3, *x_other)]
     for i, s in peers:
         pl.semaphore_signal(barrier, inc=1, device_id=to(i, s), device_id_type=MESH)
-    pairs_in = [(x_hbm, X)]
-    pairs_in += [(x_hbm.at[:, 128 * j : 128 * j + 128], X4.at[j]) for j in range(4)]
+    pairs_in = [(x_hbm.at[:, 128 * j : 128 * j + 128], X4.at[j]) for j in (1, 2)]
+    pairs_in += [(x_hbm, X)]
+    pairs_in += [(x_hbm.at[:, 128 * j : 128 * j + 128], X4.at[j]) for j in (0, 3)]
     pairs_in += [
         (jac_hbm, jac), (diss_hbm, diss), (mp_hbm, mp), (dcat_hbm, dcat), (nb_hbm, nb),
         (om_hbm, om), (ang_hbm, ang), (cnt_hbm, cnt), (met_hbm, met),
@@ -149,15 +150,10 @@
     loads = [pltpu.make_async_copy(a, b, in_sem.at[j]) for j, (a, b) in enumerate(pairs_in)]
     for copy in loads:
         copy.start()
-    for copy in loads:
-        copy.wait()
-
+    for j in range(2):
+        loads[j].wait()
     for j in range(2):
         T[:, 128 * j : 128 * j + 128] = X4[1 + j, pl.ds(0, 80, stride=4), :]
-    lane = lax.broadcasted_iota(jnp.int32, (160, 128), 1)
-    top, low = X[0:160, 0:128], X[160:320, 0:128]
-    SA[...] = jnp.where(lane < 64, top, pltpu.roll(low, 64, 1))
-    SB[...] = jnp.where(lane < 64, pltpu.roll(top, 64, 1), low)
 
     def remote(src, dst, ss, rs, i, s):
         return pltpu.make_async_remote_copy(
@@ -197,24 +193,46 @@
     def stage(src, dst, slot, s):
         return remote(src, dst, c_s.at[slot], c_r.at[slot], me, s)
 
-    hops = [
-        stage(T, TZ, 0, across),
-        stage(V, VD, 1, y_up), stage(V, VU, 2, y_dn),
-        stage(W, WD, 3, y_up3), stage(W, WU, 4, y_dn3),
-        *[stage(U, UX.at[j], 5 + j, x_other[2 - j]) for j in range(3)],
-        stage(Q, QN, 8, prv),
-    ]
+    lo, hi = pl.ds(0, 40), pl.ds(40, 40)
+
+    def ring(src, up_dst, dn_dst, slot, r, u, d):
+        return [stage(src.at[r], dn_dst.at[r], slot, u), stage(src.at[r], up_dst.at[r], slot + 1, d)]
+
+    def spread(src, slot, r):
+        return [stage(src.at[r], UX.at[j, r], slot + j, x_other[2 - j]) for j in range(3)]
+
+    across_hop = stage(T, TZ, 0, across)
+    a1, a2 = ring(V, VU, VD, 1, lo, y_up, y_dn), ring(W, WU, WD, 3, lo, y_up3, y_dn3)
+    a3 = spread(U, 5, lo)
+    b1 = spread(V, 8, hi)
+    b2, b3 = ring(U, VU, VD, 11, hi, y_up, y_dn), ring(W, WU, WD, 13, hi, y_up3, y_dn3)
+    last_hop = stage(Q, QN, 15, prv)
+
+    def begin(copies):
+        for copy in copies:
+            copy.start()
+
+    def arrive(copies):
+        for copy in copies:
+            copy.wait_recv()
+
     halo_a = remote(SA, RA, h_s.at[0], h_r.at[0], me, prv)
     halo_b = remote(SB, RB, h_s.at[1], h_r.at[1], me, nxt)
 
     pl.semaphore_wait(barrier, len(peers))
-    hops[0].start()
+    across_hop.start()
+    for copy in loads[2:]:
+        copy.wait()
 
     @pl.loop(0, STEPS)
     def _(k):
         for h in range(2):
             ex(h, k).start()
 
+    lane = lax.broadcasted_iota(jnp.int32, (160, 128), 1)
+    top, low = X4[0, 0:160], X4[0, 160:320]
+    SA[...] = jnp.where(lane < 64, top, pltpu.roll(low, 64, 1))
+    SB[...] = jnp.where(lane < 64, pltpu.roll(top, 64, 1), low)
     table = coding()
 
     def coef(name, side):
@@ -250,16 +268,27 @@
     below = jnp.bitwise_and(first + 63, 63)
     found = jnp.max(jnp.where(rel == below, 1, 0), axis=1, keepdims=True)
     off = jnp.where(found > 0, below, first)
-    offs = jnp.broadcast_to(off, (80, MORT))
+    offs = jnp.broadcast_to(off, (40, MORT))
     ox = jnp.bitwise_and(offs, 3)
     oy = jnp.bitwise_and(jnp.right_shift(offs, 2), 7)
     oz = jnp.right_shift(offs, 5)
-    shift = oy + jnp.where(xs < ox, 1, 0)
+
+    def y_moves(carry):
+        shift = oy + jnp.where(carry, 1, 0)
+        short = jnp.bitwise_and(shift, 7)
+        short = jnp.where(short > 4, short - 8, short)
+        by3 = jnp.where(short >= 2, 1, jnp.where(short <= -2, -1, 0))
+        return shift, short - 3 * by3, by3
+
+    shift, a_by1, a_by3 = y_moves(xs < ox)
+    _, b_by1, b_by3 = y_moves(xs + ox >= 4)
     flip = jnp.bitwise_and(oz + jnp.where(ys < shift, 1, 0), 1)
-    short = jnp.bitwise_and(shift, 7)
-    short = jnp.where(short > 4, short - 8, short)
-    by3 = jnp.where(short >= 2, 1, jnp.where(short <= -2, -1, 0))
-    by1 = short - 3 * by3
+
+    def three(move, ref, up_ref, dn_ref, r):
+        return jnp.where(move == 1, up_ref[r], jnp.where(move == -1, dn_ref[r], ref[r]))
+
+    def along_x(ref, r):
+        return jnp.where(ox == 0, ref[r], jnp.where(ox == 1, UX[0, r], jnp.where(ox == 2, UX[1, r], UX[2, r])))
 
     dm = diss[0, 0]
     node = lax.broadcasted_iota(jnp.int32, (64, ELS), 0)
@@ -296,11 +325,12 @@
                 for side in range(2):
                     nn(side, jnp.maximum(k - 1, 0)).start()
 
-    hops[0].wait_recv()
-    V[...] = jnp.where(flip == 1, TZ[...], T[...])
-    ACC4[...] = jnp.zeros_like(ACC4)
-    hops[1].start()
-    hops[2].start()
+    arrive([across_hop])
+    for r in (lo, hi):
+        V[r] = jnp.where(flip == 1, TZ[r], T[r])
+    ACC4[0] = jnp.zeros((ROWS, 128), f32)
+    begin(b1)
+    begin(a1)
 
     column = lax.broadcasted_iota(jnp.int32, (640, ELS), 0)
 
@@ -359,23 +389,31 @@
     halo_b.wait_recv()
     H[0:160] = jnp.where(lane < 64, RB[...], pltpu.roll(RA[...], 64, 1))
     H[160:320] = jnp.where(lane < 64, pltpu.roll(RB[...], 64, 1), RA[...])
+    for j in range(1, 4):
+        ACC4[j] = jnp.zeros((ROWS, 128), f32)
     gather_face(0)
+    arrive(a1)
+    W[lo] = three(a_by1, V, VU, VD, lo)
     gather_face(1)
-    hops[1].wait_recv()
-    hops[2].wait_recv()
-    W[...] = jnp.where(by1 == 1, VU[...], jnp.where(by1 == -1, VD[...], V[...]))
+    begin(a2)
+    arrive(b1)
+    U[hi] = along_x(V, hi)
+    relay(1, 2)
+    begin(b2)
     gather_face(2)
-    hops[3].start()
-    hops[4].start()
+    relay(2, 4)
     gather_face(3)
-    relay(1, STEPS)
+    arrive(b2)
+    W[hi] = three(b_by1, U, VU, VD, hi)
+    relay(4, STEPS)
+    begin(b3)
     gather_face(4)
     for side in range(2):
         nn(side, STEPS - 1).start()
+    arrive(a2)
+    U[lo] = three(a_by3, W, WU, WD, lo)
     gather_face(5)
-    hops[3].wait_recv()
-    hops[4].wait_recv()
-    U[...] = jnp.where(by3 == 1, WU[...], jnp.where(by3 == -1, WD[...], W[...]))
+    begin(a3)
 
     metric = met[...]
     w0 = om[0, 0]
@@ -386,23 +424,21 @@
     gain = jnp.where(live, gain, 0.0)
     drop = jnp.where(live, drop, 0.0)
     keep = jnp.where(live, 1.0, 0.0)
-    for j in range(3):
-        hops[5 + j].start()
     remote(X, XP, ex_s, ex_r.at[0, 0], mate, sp).wait_send()
     for side in range(2):
         mm_sent(side).wait_send()
-    for j in range(3):
-        hops[5 + j].wait_recv()
-    Q[...] = jnp.where(ox == 0, U[...], jnp.where(ox == 1, UX[0], jnp.where(ox == 2, UX[1], UX[2])))
     turn = jnp.full((16, MORT), ang[0, 0], f32)
     cosine, sine = jnp.cos(turn), jnp.sin(turn)
     index = jnp.bitwise_and(rel - off + 64, 63) * MORT + jnp.bitwise_and(pairs, MORT - 1)
     hot = jnp.where(lax.broadcasted_iota(jnp.int32, (2 * MORT, MORT), 0) == index, 1.0, 0.0).astype(bf16)
-    hops[8].start()
-    for copy in (*hops[:8], halo_a, halo_b):
+    arrive(b3)
+    Q[hi] = three(b_by3, W, WU, WD, hi)
+    arrive(a3)
+    Q[lo] = along_x(U, lo)
+    for copy in (across_hop, *a1, *a2, *b1, *b2, *b3, *a3, halo_a, halo_b):
         copy.wait_send()
-
-    hops[8].wait_recv()
+    last_hop.start()
+    arrive([last_hop])
     window = jnp.concatenate([Q[...], QN[...]], axis=1)
     high, low = split(window)
     both = jnp.dot(jnp.concatenate([high, low], axis=0), hot, preferred_element_type=f32)
@@ -421,12 +457,6 @@
             face = jnp.concatenate([ACC4[j, r] for j in range(4)], axis=1)
             ACC[r] = keep * X[r] + gain * (ACC[r] + face) - drop * combine(("bo", "bp", "fm"), (X, XP, MR), side, r)
 
-    def finish(k):
-        for side in range(2):
-            ee(1 - side, k).wait_recv()
-            r = rows(side, k)
-            out[r] = ACC[r] - drop * (coef("fn", side) * NR[r] + ER[r])
-
     @pl.loop(0, STEPS)
     def _(k):
         for side in range(2):
@@ -436,17 +466,34 @@
 
         @pl.when(k > 0)
         def _():
-            finish(jnp.maximum(k - 1, 0))
-
-        for side in range(2):
-            ee(side, k).start()
-
-    hops[8].wait_send()
+            for side in range(2):
+                ee(side, jnp.maximum(k - 1, 0)).start()
+
+    last_hop.wait_send()
     for side in range(2):
         nn_sent(side).wait_send()
-    finish(STEPS - 1)
+    for side in range(2):
+        ee(side, STEPS - 1).start()
+
+    def put(side, k):
+        r = rows(side, k)
+        return pltpu.make_async_copy(OUT.at[r], out.at[r], out_sem.at[side, k])
+
+    @pl.loop(0, STEPS)
+    def _(k):
+        for side in range(2):
+            ee(1 - side, k).wait_recv()
+            r = rows(side, k)
+            OUT[r] = ACC[r] - drop * (coef("fn", side) * NR[r] + ER[r])
+            put(side, k).start()
+
     for side in range(2):
         ee_sent(side).wait_send()
+
+    @pl.loop(0, STEPS)
+    def _(k):
+        for side in range(2):
+            put(side, k).wait()
 
 
 def shards(state, metric, jacobians, dissipation, omega, rotor_angle, counts, neighbours, mortar_pairs):
@@ -472,8 +519,8 @@
         kernel,
         out_shape=jax.ShapeDtypeStruct((ROWS, ELS), f32),
         in_specs=[pl.BlockSpec(memory_space=pltpu.VMEM) if a.size == 1 else anywhere for a in operands],
-        out_specs=pl.BlockSpec(memory_space=pltpu.VMEM),
-        scratch_shapes=[whole] * 9
+        out_specs=pl.BlockSpec(memory_space=pl.ANY),
+        scratch_shapes=[whole] * 10
         + [pltpu.VMEM((4, ROWS, 128), f32)] * 2
         + [quarter] * 4
         + [pltpu.VMEM((ROWS, 128), f32)]
@@ -487,7 +534,8 @@
         + [sem((14,)), sem(()), sem((2, STEPS))]
         + [sem((2,)), sem((2, STEPS))] * 3
         + [sem((2,))] * 2
-        + [sem((9,))] * 2,
+        + [sem((16,))] * 2
+        + [sem((2, STEPS))],
         compiler_params=pltpu.CompilerParams(collective_id=0, has_side_effects=True, vmem_limit_bytes=VMEM_BYTES),
         name="step",
     )(

time: 60.7 us -> 55.8 us (0.919)
  Pallas kernels: 57.1 us -> 52.2 us
    pallas_call x1, Pallas kernels: 57.1 us -> 52.2 us  [shards(): pl.pallas_call(kernel, out_shape=jax.ShapeDtypeStruct((ROWS, ELS), f32),...]
where the time goes in v3:
time: 55.8 us; the launch traced here: 55.6 us
  Pallas kernels  52.2 us (94%)
  between operations  2.59 us (5%)
  local copies, waits for them, and re-layouts  0.84 us (2%)
    pallas_call x1, Pallas kernels, shards(): pl.pallas_call(kernel, out_shape=jax.ShapeDtypeStruct((ROWS, ELS), f32),...  52.2 us

profile of v3, /device:TPU:1, one launch (start us, length us, event | category | flops | bytes accessed | tf_op | source)
XLA Modules:
  0.0 55.6 jit_solution(10253324940686960522)
XLA Ops:
  2.6 52.2 %step.1 = f32[320,512]{1,0:T(8,128)S(1)} custom-call(f32[320,512]{1,0:T(8,128)} %bitcast.13, f32[1,512]{1,0:T(1,128)} %bitcast.15, f32[5,3,5]{2,1,0:T(4,128)} %bitcast.14, f32[1,1]{1,0:T(1,128)} %bitcast.8.diss_hbm, f32[1,1]{1,0:T(1,128)} %bitcast.9.om_hbm, f32[1,1]{1,0:T(1,128)} %bitcast.10.ang_hbm, s32[1,1]{1,0:T(1,128)} %bitcast.11.cnt_hbm, ...), custom_call_target="tpu_custom_call" | custom-call | tf_op jit(solution)/shard_map/step/pallas_call | solution.py:518
  54.8 0.8 %copy.16 = f32[1,5,64,512]{3,2,1,0:T(8,128)} copy(f32[1,5,64,512]{3,2,1,0:T(8,128)S(1)} %bitcast.12) | data formatting | bytes 1310720

commit v4 on v3

--- a/solution.py
+++ b/solution.py
@@ -191,7 +191,7 @@
     ee, ee_sent = flow(ES, ER, e_s, e_r, None)
 
     def stage(src, dst, slot, s):
-        return remote(src, dst, c_s.at[slot], c_r.at[slot], me, s)
+        return remote(src, dst, c_s.at[slot // 15], c_r.at[slot], me, s)
 
     lo, hi = pl.ds(0, 40), pl.ds(40, 40)
 
@@ -206,7 +206,8 @@
     a3 = spread(U, 5, lo)
     b1 = spread(V, 8, hi)
     b2, b3 = ring(U, VU, VD, 11, hi, y_up, y_dn), ring(W, WU, WD, 13, hi, y_up3, y_dn3)
-    last_hop = stage(Q, QN, 15, prv)
+    last_lo = stage(Q.at[lo], QN.at[lo], 15, prv)
+    last_hi = stage(Q.at[hi], QN.at[hi], 16, prv)
 
     def begin(copies):
         for copy in copies:
@@ -216,8 +217,8 @@
         for copy in copies:
             copy.wait_recv()
 
-    halo_a = remote(SA, RA, h_s.at[0], h_r.at[0], me, prv)
-    halo_b = remote(SB, RB, h_s.at[1], h_r.at[1], me, nxt)
+    halo_a = remote(SA, RA, h_s, h_r.at[0], me, prv)
+    halo_b = remote(SB, RB, h_s, h_r.at[1], me, nxt)
 
     pl.semaphore_wait(barrier, len(peers))
     across_hop.start()
@@ -401,19 +402,17 @@
     relay(1, 2)
     begin(b2)
     gather_face(2)
-    relay(2, 4)
     gather_face(3)
     arrive(b2)
     W[hi] = three(b_by1, U, VU, VD, hi)
-    relay(4, STEPS)
+    gather_face(4)
     begin(b3)
-    gather_face(4)
-    for side in range(2):
-        nn(side, STEPS - 1).start()
+    relay(2, 4)
     arrive(a2)
     U[lo] = three(a_by3, W, WU, WD, lo)
     gather_face(5)
     begin(a3)
+    relay(4, STEPS)
 
     metric = met[...]
     w0 = om[0, 0]
@@ -424,21 +423,49 @@
     gain = jnp.where(live, gain, 0.0)
     drop = jnp.where(live, drop, 0.0)
     keep = jnp.where(live, 1.0, 0.0)
-    remote(X, XP, ex_s, ex_r.at[0, 0], mate, sp).wait_send()
     for side in range(2):
-        mm_sent(side).wait_send()
+        nn(side, STEPS - 1).start()
+    def face_base():
+        @pl.loop(0, STEPS)
+        def _(k):
+            for side in range(2):
+                r = rows(side, k)
+                ACC[r] = keep * X[r] + gain * ACC[r] - drop * combine(("bo", "bp", "fm"), (X, XP, MR), side, r)
+
     turn = jnp.full((16, MORT), ang[0, 0], f32)
     cosine, sine = jnp.cos(turn), jnp.sin(turn)
     index = jnp.bitwise_and(rel - off + 64, 63) * MORT + jnp.bitwise_and(pairs, MORT - 1)
     hot = jnp.where(lax.broadcasted_iota(jnp.int32, (2 * MORT, MORT), 0) == index, 1.0, 0.0).astype(bf16)
+    remote(X, XP, ex_s, ex_r.at[0, 0], mate, sp).wait_send()
+    for side in range(2):
+        mm_sent(side).wait_send()
     arrive(b3)
     Q[hi] = three(b_by3, W, WU, WD, hi)
+    face_base()
+    begin([last_hi])
     arrive(a3)
     Q[lo] = along_x(U, lo)
-    for copy in (across_hop, *a1, *a2, *b1, *b2, *b3, *a3, halo_a, halo_b):
-        copy.wait_send()
-    last_hop.start()
-    arrive([last_hop])
+    remote(X, XP, c_s.at[0], ex_r.at[0, 0], mate, sp).wait_send()
+    remote(H, H, h_s, h_r.at[0], me, prv).wait_send()
+    begin([last_lo])
+
+    @pl.loop(0, STEPS)
+    def _(k):
+        for side in range(2):
+            nn(side, k).wait_recv()
+            r = rows(side, k)
+            ES[r] = combine(("em", "en"), (MR, NR), side, r)
+
+        @pl.when(k > 0)
+        def _():
+            for side in range(2):
+                ee(side, jnp.maximum(k - 1, 0)).start()
+
+    for side in range(2):
+        nn_sent(side).wait_send()
+    for side in range(2):
+        ee(side, STEPS - 1).start()
+    arrive([last_hi, last_lo])
     window = jnp.concatenate([Q[...], QN[...]], axis=1)
     high, low = split(window)
     both = jnp.dot(jnp.concatenate([high, low], axis=0), hot, preferred_element_type=f32)
@@ -450,50 +477,24 @@
         for j in range(2):
             ACC4[1 + j, pl.ds(64 * g + 3, 16, stride=4), :] += part[:, 128 * j : 128 * j + 128]
 
-    @pl.loop(0, STEPS)
-    def _(k):
-        for side in range(2):
-            r = rows(side, k)
-            face = jnp.concatenate([ACC4[j, r] for j in range(4)], axis=1)
-            ACC[r] = keep * X[r] + gain * (ACC[r] + face) - drop * combine(("bo", "bp", "fm"), (X, XP, MR), side, r)
-
-    @pl.loop(0, STEPS)
-    def _(k):
-        for side in range(2):
-            nn(side, k).wait_recv()
-            r = rows(side, k)
-            ES[r] = combine(("em", "en"), (MR, NR), side, r)
-
-        @pl.when(k > 0)
-        def _():
-            for side in range(2):
-                ee(side, jnp.maximum(k - 1, 0)).start()
-
-    last_hop.wait_send()
-    for side in range(2):
-        nn_sent(side).wait_send()
-    for side in range(2):
-        ee(side, STEPS - 1).start()
-
     def put(side, k):
         r = rows(side, k)
-        return pltpu.make_async_copy(OUT.at[r], out.at[r], out_sem.at[side, k])
+        return pltpu.make_async_copy(OUT.at[r], out.at[r], out_sem)
 
     @pl.loop(0, STEPS)
     def _(k):
         for side in range(2):
             ee(1 - side, k).wait_recv()
             r = rows(side, k)
-            OUT[r] = ACC[r] - drop * (coef("fn", side) * NR[r] + ER[r])
+            face = jnp.concatenate([ACC4[j, r] for j in range(4)], axis=1)
+            OUT[r] = ACC[r] + gain * face - drop * (coef("fn", side) * NR[r] + ER[r])
             put(side, k).start()
 
     for side in range(2):
         ee_sent(side).wait_send()
 
-    @pl.loop(0, STEPS)
-    def _(k):
-        for side in range(2):
-            put(side, k).wait()
+    remote(Q, QN, c_s.at[1], c_r.at[15], me, prv).wait_send()
+    pltpu.make_async_copy(OUT, out, out_sem).wait()
 
 
 def shards(state, metric, jacobians, dissipation, omega, rotor_angle, counts, neighbours, mortar_pairs):
@@ -533,9 +534,9 @@
         + [pltpu.SMEM((1, 1), jnp.int32)]
         + [sem((14,)), sem(()), sem((2, STEPS))]
         + [sem((2,)), sem((2, STEPS))] * 3
-        + [sem((2,))] * 2
-        + [sem((16,))] * 2
-        + [sem((2, STEPS))],
+        + [sem(()), sem((2,))]
+        + [sem((2,)), sem((17,))]
+        + [sem(())],
         compiler_params=pltpu.CompilerParams(collective_id=0, has_side_effects=True, vmem_limit_bytes=VMEM_BYTES),
         name="step",
     )(

time: 55.8 us -> 53.8 us (0.964)
  Pallas kernels: 52.2 us -> 50.2 us
    pallas_call x1, Pallas kernels: 52.2 us -> 50.2 us  [shards(): pl.pallas_call(kernel, out_shape=jax.ShapeDtypeStruct((ROWS, ELS), f32),...]
where the time goes in v4:
time: 53.8 us; the launch traced here: 53.7 us
  Pallas kernels  50.2 us (93%)
  between operations  2.59 us (5%)
  local copies, waits for them, and re-layouts  0.84 us (2%)
    pallas_call x1, Pallas kernels, shards(): pl.pallas_call(kernel, out_shape=jax.ShapeDtypeStruct((ROWS, ELS), f32),...  50.2 us

profile of v4, /device:TPU:1, one launch (start us, length us, event | category | flops | bytes accessed | tf_op | source)
XLA Modules:
  0.0 53.7 jit_solution(5563545831220915114)
XLA Ops:
  2.6 50.2 %step.1 = f32[320,512]{1,0:T(8,128)S(1)} custom-call(f32[320,512]{1,0:T(8,128)} %bitcast.13, f32[1,512]{1,0:T(1,128)} %bitcast.15, f32[5,3,5]{2,1,0:T(4,128)} %bitcast.14, f32[1,1]{1,0:T(1,128)} %bitcast.8.diss_hbm, f32[1,1]{1,0:T(1,128)} %bitcast.9.om_hbm, f32[1,1]{1,0:T(1,128)} %bitcast.10.ang_hbm, s32[1,1]{1,0:T(1,128)} %bitcast.11.cnt_hbm, ...), custom_call_target="tpu_custom_call" | custom-call | tf_op jit(solution)/shard_map/step/pallas_call | solution.py:519
  52.8 0.8 %copy.16 = f32[1,5,64,512]{3,2,1,0:T(8,128)} copy(f32[1,5,64,512]{3,2,1,0:T(8,128)S(1)} %bitcast.12) | data formatting | bytes 1310720

commit v5 on v4

--- a/solution.py
+++ b/solution.py
@@ -13,7 +13,7 @@
 MORT = 256
 ROWS = 320
 ELS = 512
-STEPS = 5
+STEPS = 4
 PIECE = ROWS // 2 // STEPS
 VMEM_BYTES = 24 * 2**20
 MESH = pl.DeviceIdType.MESH
@@ -184,7 +184,7 @@
 
     def ex(h, k):
         r = plain(k, h)
-        return remote(X.at[r], XP.at[r], ex_s, ex_r.at[h, k], mate, sp)
+        return remote(x_hbm.at[r], XP.at[r], ex_s, ex_r.at[h, k], mate, sp)
 
     mm, mm_sent = flow(MS, MR, m_s, m_r, (up, down))
     nn, nn_sent = flow(NS, NR, n_s, n_r, (up, down))
@@ -222,18 +222,15 @@
 
     pl.semaphore_wait(barrier, len(peers))
     across_hop.start()
-    for copy in loads[2:]:
-        copy.wait()
 
     @pl.loop(0, STEPS)
     def _(k):
         for h in range(2):
             ex(h, k).start()
 
-    lane = lax.broadcasted_iota(jnp.int32, (160, 128), 1)
-    top, low = X4[0, 0:160], X4[0, 160:320]
-    SA[...] = jnp.where(lane < 64, top, pltpu.roll(low, 64, 1))
-    SB[...] = jnp.where(lane < 64, pltpu.roll(top, 64, 1), low)
+    for copy in loads[2:]:
+        copy.wait()
+
     table = coding()
 
     def coef(name, side):
@@ -258,10 +255,14 @@
             for side in range(2):
                 mm(side, jnp.maximum(k - 1, 0)).start()
 
+    lane = lax.broadcasted_iota(jnp.int32, (160, 128), 1)
+    top, low = X4[0, 0:160], X4[0, 160:320]
+    SA[...] = jnp.where(lane < 64, top, pltpu.roll(low, 64, 1))
+    SB[...] = jnp.where(lane < 64, pltpu.roll(top, 64, 1), low)
+    for side in range(2):
+        mm(side, STEPS - 1).start()
     halo_a.start()
     halo_b.start()
-    for side in range(2):
-        mm(side, STEPS - 1).start()
 
     pairs = mp[...]
     rel = jnp.bitwise_and(jnp.right_shift(pairs, 8) - sp + 64, 63)
@@ -385,7 +386,6 @@
                 for j in range(4):
                     ACC4[j, pl.ds(64 * g + end, 16, stride=4), :] = part[:, 128 * j : 128 * j + 128]
 
-    relay(0, 1)
     halo_a.wait_recv()
     halo_b.wait_recv()
     H[0:160] = jnp.where(lane < 64, RB[...], pltpu.roll(RA[...], 64, 1))
@@ -399,20 +399,20 @@
     begin(a2)
     arrive(b1)
     U[hi] = along_x(V, hi)
-    relay(1, 2)
     begin(b2)
+    relay(0, 2)
     gather_face(2)
     gather_face(3)
     arrive(b2)
     W[hi] = three(b_by1, U, VU, VD, hi)
     gather_face(4)
     begin(b3)
-    relay(2, 4)
+    relay(2, 3)
     arrive(a2)
     U[lo] = three(a_by3, W, WU, WD, lo)
     gather_face(5)
     begin(a3)
-    relay(4, STEPS)
+    relay(3, STEPS)
 
     metric = met[...]
     w0 = om[0, 0]
@@ -436,7 +436,7 @@
     cosine, sine = jnp.cos(turn), jnp.sin(turn)
     index = jnp.bitwise_and(rel - off + 64, 63) * MORT + jnp.bitwise_and(pairs, MORT - 1)
     hot = jnp.where(lax.broadcasted_iota(jnp.int32, (2 * MORT, MORT), 0) == index, 1.0, 0.0).astype(bf16)
-    remote(X, XP, ex_s, ex_r.at[0, 0], mate, sp).wait_send()
+    remote(x_hbm, XP, ex_s, ex_r.at[0, 0], mate, sp).wait_send()
     for side in range(2):
         mm_sent(side).wait_send()
     arrive(b3)

time: 53.8 us -> 53.9 us (level)
  the two profiles are of different devices: /device:TPU:1 before, /device:TPU:57 now
where the time goes in v5:
time: 53.9 us; the launch traced here: 53.8 us
  Pallas kernels  50.3 us (93%)
  between operations  2.59 us (5%)
  local copies, waits for them, and re-layouts  0.84 us (2%)
    pallas_call x1, Pallas kernels, shards(): pl.pallas_call(kernel, out_shape=jax.ShapeDtypeStruct((ROWS, ELS), f32),...  50.3 us

profile of v5, /device:TPU:57, one launch (start us, length us, event | category | flops | bytes accessed | tf_op | source)
XLA Modules:
  0.0 53.8 jit_solution(5899475404530305943)
XLA Ops:
  2.6 50.3 %step.1 = f32[320,512]{1,0:T(8,128)S(1)} custom-call(f32[320,512]{1,0:T(8,128)} %bitcast.13, f32[1,512]{1,0:T(1,128)} %bitcast.15, f32[5,3,5]{2,1,0:T(4,128)} %bitcast.14, f32[1,1]{1,0:T(1,128)} %bitcast.8.diss_hbm, f32[1,1]{1,0:T(1,128)} %bitcast.9.om_hbm, f32[1,1]{1,0:T(1,128)} %bitcast.10.ang_hbm, s32[1,1]{1,0:T(1,128)} %bitcast.11.cnt_hbm, ...), custom_call_target="tpu_custom_call" | custom-call | tf_op jit(solution)/shard_map/step/pallas_call | solution.py:519
  52.9 0.8 %copy.16 = f32[1,5,64,512]{3,2,1,0:T(8,128)} copy(f32[1,5,64,512]{3,2,1,0:T(8,128)S(1)} %bitcast.12) | data formatting | bytes 1310720
